TPU v7x, 32 devices: a whole 2x2x4 slice. The times are simulated.
32 devices in a mesh: dp: 8 (over z, y), head: 4 (over x, core).
Axes of the slice: x: 2, y: 2, z: 4, core: 2. Of those that a mesh axis runs over, the one named last changes fastest.
Arguments:
- source: bfloat16 [2, 16384, 512], P(None, ('dp', 'head')), may hold values from -6 to 6
- target: bfloat16 [2, 16384, 512], P(None, ('dp', 'head')), may hold values from -6 to 6
- cotangent: bfloat16 [2, 16384, 512], P(None, ('dp', 'head')), may hold values from -6 to 6
- short_lengths: int32 [2, 64], P(None, 'dp'), may hold values from 128 to 256, as said below
- long_lengths: int32 [2, 16], P(None, 'dp'), may hold values from 512 to 1024, as said below
- attn_weights: bfloat16 [12, 512, 512], replicated, may hold values from -0.375 to 0.375
- up_weights: bfloat16 [2, 512, 2048], replicated, may hold values from -0.25 to 0.25
- down_weights: bfloat16 [2, 2048, 512], replicated, may hold values from -0.125 to 0.125
- norm_gains: float32 [5, 512], replicated, may hold values from 0.25 to 1.75
- norm_shifts: float32 [5, 512], replicated, may hold values from -1 to 1
Outputs:
- decoded: bfloat16 [2, 16384, 512], P(None, ('dp', 'head'))
- grad_source: float32 [2, 16384, 512], P(None, ('dp', 'head'))
- grad_target: float32 [2, 16384, 512], P(None, ('dp', 'head'))
- grad_attn: float32 [12, 512, 512], P(None, ('dp', 'head'))
- grad_up: float32 [2, 512, 2048], P(None, ('dp', 'head'))
- grad_down: float32 [2, 2048, 512], P(None, ('dp', 'head'))
- grad_gains: float32 [5, 512], P(None, ('dp', 'head'))
- grad_shifts: float32 [5, 512], P(None, ('dp', 'head'))
Inputs may be any that keep to these rules, and one draw needn't show every extreme that they name: `short_lengths`: row 0 holds the source lengths and row 1 the target lengths of the 64 slots, in slot order; each row has a slot of exactly 256. `long_lengths`: row 0 holds the source lengths and row 1 the target lengths of the 16 slots, in slot order; each row has a slot of exactly 1024.
All inputs are finite; a program needn't handle non-finite values.
Results may differ from a plain program's by a relative error of at most 0.025.
The roundings to bfloat16 on the way count: a program that leaves them out, or rounds other values in their place, can miss the bound.
Values may be sent and summed in bfloat16 or wider, within the bound.
A program may use at most 320 MiB of HBM per device.

v0:
```python
import math

import jax
import jax.numpy as jnp
from jax import lax
from jax.sharding import PartitionSpec as P

HEADS = 8
SHORT = 256
LONG = 1024


EPSILON = 1e-05
MASKED = -1e30


def layer_norm(residual, gain, shift):
    average = jnp.mean(residual, axis=-1, keepdims=True)
    centered = residual - average
    variance = jnp.mean(centered * centered, axis=-1, keepdims=True)
    return centered * lax.rsqrt(variance + EPSILON) * gain + shift


def norm_backward(residual, gain, shift, gradient):
    unused, pullback = jax.vjp(layer_norm, residual, gain, shift)
    return pullback(gradient)


def matmul(operand, weight):
    return jnp.dot(operand, weight, preferred_element_type=jnp.float32)


def left_grad(gradient, weight):
    return lax.dot_general(
        gradient, weight, (((1,), (1,)), ((), ())), preferred_element_type=jnp.float32
    )


def weight_grad(operand, gradient):
    return lax.dot_general(
        operand, gradient, (((0,), (0,)), ((), ())), preferred_element_type=jnp.float32
    )


def live_mask(lengths, slot_size):
    return (jnp.arange(slot_size)[None, :] < lengths[:, None]).reshape(-1)


def split_heads(flat):
    groups = lax.axis_size("head")
    return flat.reshape(flat.shape[0], groups, HEADS // groups, -1)


def slot_scores(query_rows, key_rows, key_live, causal, slot_size, score_scale):
    scores = (
        jnp.einsum("aqhd,akhd->ahqk", query_rows, key_rows, preferred_element_type=jnp.float32)
        * score_scale
    )
    allowed = key_live[:, None, None, :]
    if causal:
        position = jnp.arange(slot_size)
        allowed = allowed & (position[None, :] <= position[:, None])[None, None, :, :]
    return jnp.where(allowed, scores, MASKED)


def attend_forward(query_head, key_head, value_head, key_live, causal, slot_size):
    total_rows = query_head.shape[0]
    heads_here = query_head.shape[2]
    head_dim = query_head.shape[3]
    block_count = total_rows // LONG
    slot_count = LONG // slot_size
    score_scale = 1.0 / math.sqrt(head_dim)
    slot_shape = (slot_count, slot_size, heads_here, head_dim)

    def one_block(pieces):
        query_rows, key_rows, value_rows, live_rows = pieces
        scores = slot_scores(
            query_rows.reshape(slot_shape),
            key_rows.reshape(slot_shape),
            live_rows.reshape(slot_count, slot_size),
            causal,
            slot_size,
            score_scale,
        )
        highest = jnp.max(scores, axis=-1, keepdims=True)
        powers = jnp.exp(scores - highest)
        totals = jnp.sum(powers, axis=-1, keepdims=True)
        softmax_low = (powers / totals).astype(jnp.bfloat16)
        output = jnp.einsum(
            "ahqk,akhd->aqhd",
            softmax_low,
            value_rows.reshape(slot_shape),
            preferred_element_type=jnp.float32,
        )
        logsum = jnp.transpose((highest + jnp.log(totals))[..., 0], (0, 2, 1))
        return (
            output.astype(jnp.bfloat16).reshape(LONG, 1, heads_here, head_dim),
            logsum.reshape(LONG, 1, heads_here),
        )

    block_shape = (block_count, LONG, heads_here, head_dim)
    outputs, logsums = lax.map(
        one_block,
        (
            query_head.reshape(block_shape),
            key_head.reshape(block_shape),
            value_head.reshape(block_shape),
            key_live.reshape(block_count, LONG),
        ),
    )
    return (
        outputs.reshape(total_rows, 1, heads_here, head_dim),
        logsums.reshape(total_rows, 1, heads_here),
    )


def attend_backward(
    query_head, key_head, value_head, logsum, grad_head, key_live, causal, slot_size
):
    total_rows = query_head.shape[0]
    heads_here = query_head.shape[2]
    head_dim = query_head.shape[3]
    block_count = total_rows // LONG
    slot_count = LONG // slot_size
    score_scale = 1.0 / math.sqrt(head_dim)
    slot_shape = (slot_count, slot_size, heads_here, head_dim)
    final_shape = (LONG, 1, heads_here, head_dim)

    def one_block(pieces):
        query_rows, key_rows, value_rows, logsum_rows, grad_rows, live_rows = pieces
        query_rows = query_rows.reshape(slot_shape)
        key_rows = key_rows.reshape(slot_shape)
        value_rows = value_rows.reshape(slot_shape)
        grad_rows = grad_rows.reshape(slot_shape)
        scores = slot_scores(
            query_rows,
            key_rows,
            live_rows.reshape(slot_count, slot_size),
            causal,
            slot_size,
            score_scale,
        )
        logsum_here = jnp.transpose(
            logsum_rows.reshape(slot_count, slot_size, heads_here), (0, 2, 1)
        )[..., None]
        probs_full = jnp.exp(scores - logsum_here)
        grad_value = jnp.einsum(
            "ahqk,aqhd->akhd",
            probs_full.astype(jnp.bfloat16),
            grad_rows,
            preferred_element_type=jnp.float32,
        )
        grad_probs = jnp.einsum(
            "aqhd,akhd->ahqk", grad_rows, value_rows, preferred_element_type=jnp.float32
        )
        row_inner = jnp.sum(probs_full * grad_probs, axis=-1, keepdims=True)
        grad_scores = (probs_full * (grad_probs - row_inner)).astype(jnp.bfloat16)
        grad_query = (
            jnp.einsum("ahqk,akhd->aqhd", grad_scores, key_rows, preferred_element_type=jnp.float32)
            * score_scale
        )
        grad_key = (
            jnp.einsum(
                "ahqk,aqhd->akhd", grad_scores, query_rows, preferred_element_type=jnp.float32
            )
            * score_scale
        )
        return tuple(
            (
                member.astype(jnp.bfloat16).reshape(final_shape)
                for member in (grad_query, grad_key, grad_value)
            )
        )

    block_shape = (block_count, LONG, heads_here, head_dim)
    results = lax.map(
        one_block,
        (
            query_head.reshape(block_shape),
            key_head.reshape(block_shape),
            value_head.reshape(block_shape),
            logsum.reshape(block_count, LONG, heads_here),
            grad_head.reshape(block_shape),
            key_live.reshape(block_count, LONG),
        ),
    )
    return tuple((member.reshape(total_rows, 1, heads_here, head_dim) for member in results))


def attention_forward(rows_query, rows_source, weights, base_index, key_live, causal, slot_size):
    row_count = rows_query.shape[0]
    query_flat = matmul(rows_query, weights[base_index]).astype(jnp.bfloat16)
    key_flat = matmul(rows_source, weights[base_index + 1]).astype(jnp.bfloat16)
    value_flat = matmul(rows_source, weights[base_index + 2]).astype(jnp.bfloat16)
    pieces = (
        lax.all_to_all(split_heads(query_flat), "head", split_axis=1, concat_axis=0, tiled=True),
        lax.all_to_all(split_heads(key_flat), "head", split_axis=1, concat_axis=0, tiled=True),
        lax.all_to_all(split_heads(value_flat), "head", split_axis=1, concat_axis=0, tiled=True),
    )
    output_head, logsum = attend_forward(
        pieces[0], pieces[1], pieces[2], key_live, causal, slot_size
    )
    merged = lax.all_to_all(output_head, "head", split_axis=0, concat_axis=1, tiled=True).reshape(
        row_count, -1
    )
    branch = matmul(merged, weights[base_index + 3])
    return (branch, (merged, logsum, pieces[0], pieces[1], pieces[2]))


def attention_backward(
    saved, grad_branch, weights, base_index, rows_query, rows_source, key_live, causal, slot_size
):
    merged, logsum, query_head, key_head, value_head = saved
    row_count = grad_branch.shape[0]
    grad_out_weight = weight_grad(merged, grad_branch)
    grad_merged = left_grad(grad_branch, weights[base_index + 3]).astype(jnp.bfloat16)
    grad_head = lax.all_to_all(
        split_heads(grad_merged), "head", split_axis=1, concat_axis=0, tiled=True
    )
    grad_query, grad_key, grad_value = attend_backward(
        query_head, key_head, value_head, logsum, grad_head, key_live, causal, slot_size
    )
    back_query, back_key, back_value = (
        lax.all_to_all(grad_query, "head", split_axis=0, concat_axis=1, tiled=True),
        lax.all_to_all(grad_key, "head", split_axis=0, concat_axis=1, tiled=True),
        lax.all_to_all(grad_value, "head", split_axis=0, concat_axis=1, tiled=True),
    )
    back_query = back_query.reshape(row_count, -1)
    back_key = back_key.reshape(row_count, -1)
    back_value = back_value.reshape(row_count, -1)
    grad_query_in = left_grad(back_query, weights[base_index])
    grad_source_in = left_grad(back_key, weights[base_index + 1]) + left_grad(
        back_value, weights[base_index + 2]
    )
    stacked = jnp.stack(
        [
            weight_grad(rows_query, back_query),
            weight_grad(rows_source, back_key),
            weight_grad(rows_source, back_value),
            grad_out_weight,
        ]
    )
    return (grad_query_in, grad_source_in, stacked)


def feed_forward(hidden_low, up_weight, down_weight):
    upward = matmul(hidden_low, up_weight)
    activated = jax.nn.silu(upward).astype(jnp.bfloat16)
    return (matmul(activated, down_weight), (upward, activated))


def feed_backward(hidden_low, saved, gradient_low, up_weight, down_weight):
    upward, activated = saved
    grad_down = weight_grad(activated, gradient_low)
    grad_activated = left_grad(gradient_low, down_weight)
    unused, pullback = jax.vjp(jax.nn.silu, upward)
    grad_upward = pullback(grad_activated)[0].astype(jnp.bfloat16)
    return (left_grad(grad_upward, up_weight), weight_grad(hidden_low, grad_upward), grad_down)


def encoder_forward(source_rows, attn, ups, downs, gains, shifts, live_source, slot_size):
    branch, attn_saved = attention_forward(
        source_rows, source_rows, attn, 0, live_source, False, slot_size
    )
    first_resid = source_rows.astype(jnp.float32) + branch
    first_hidden = layer_norm(first_resid, gains[0], shifts[0])
    first_low = first_hidden.astype(jnp.bfloat16)
    ffn_branch, ffn_saved = feed_forward(first_low, ups[0], downs[0])
    second_resid = first_hidden + ffn_branch
    encoded = layer_norm(second_resid, gains[1], shifts[1])
    return (encoded, (source_rows, attn_saved, first_resid, first_low, ffn_saved, second_resid))


def encoder_backward(saved, grad_encoded, attn, ups, downs, gains, shifts, live_source, slot_size):
    source_rows, attn_saved, first_resid, first_low, ffn_saved, second_resid = saved
    grad_second, gain_two, shift_two = norm_backward(
        second_resid, gains[1], shifts[1], grad_encoded
    )
    grad_hidden, grad_up, grad_down = feed_backward(
        first_low, ffn_saved, grad_second.astype(jnp.bfloat16), ups[0], downs[0]
    )
    grad_first, gain_one, shift_one = norm_backward(
        first_resid, gains[0], shifts[0], grad_second + grad_hidden
    )
    grad_query_in, grad_source_in, attn_grads = attention_backward(
        attn_saved,
        grad_first.astype(jnp.bfloat16),
        attn,
        0,
        source_rows,
        source_rows,
        live_source,
        False,
        slot_size,
    )
    grad_source = grad_first + grad_query_in + grad_source_in
    return (
        grad_source,
        (attn_grads, grad_up, grad_down, (gain_one, gain_two), (shift_one, shift_two)),
    )


def decoder_forward(
    target_rows, encoded_low, attn, ups, downs, gains, shifts, live_source, live_target, slot_size
):
    self_branch, self_saved = attention_forward(
        target_rows, target_rows, attn, 4, live_target, True, slot_size
    )
    first_resid = target_rows.astype(jnp.float32) + self_branch
    first_hidden = layer_norm(first_resid, gains[2], shifts[2])
    first_low = first_hidden.astype(jnp.bfloat16)
    cross_branch, cross_saved = attention_forward(
        first_low, encoded_low, attn, 8, live_source, False, slot_size
    )
    second_resid = first_hidden + cross_branch
    second_hidden = layer_norm(second_resid, gains[3], shifts[3])
    second_low = second_hidden.astype(jnp.bfloat16)
    ffn_branch, ffn_saved = feed_forward(second_low, ups[1], downs[1])
    third_resid = second_hidden + ffn_branch
    decoded = layer_norm(third_resid, gains[4], shifts[4])
    return (
        decoded,
        (
            target_rows,
            encoded_low,
            self_saved,
            first_resid,
            first_low,
            cross_saved,
            second_resid,
            second_low,
            ffn_saved,
            third_resid,
        ),
    )


def decoder_backward(
    saved, cot_rows, attn, ups, downs, gains, shifts, live_source, live_target, slot_size
):
    (
        target_rows,
        encoded_low,
        self_saved,
        first_resid,
        first_low,
        cross_saved,
        second_resid,
        second_low,
        ffn_saved,
        third_resid,
    ) = saved
    grad_third, gain_five, shift_five = norm_backward(third_resid, gains[4], shifts[4], cot_rows)
    grad_hidden, grad_up, grad_down = feed_backward(
        second_low, ffn_saved, grad_third.astype(jnp.bfloat16), ups[1], downs[1]
    )
    grad_second, gain_four, shift_four = norm_backward(
        second_resid, gains[3], shifts[3], grad_third + grad_hidden
    )
    grad_cross_query, grad_encoded, cross_grads = attention_backward(
        cross_saved,
        grad_second.astype(jnp.bfloat16),
        attn,
        8,
        first_low,
        encoded_low,
        live_source,
        False,
        slot_size,
    )
    grad_first, gain_three, shift_three = norm_backward(
        first_resid, gains[2], shifts[2], grad_second + grad_cross_query
    )
    grad_self_query, grad_self_source, self_grads = attention_backward(
        self_saved,
        grad_first.astype(jnp.bfloat16),
        attn,
        4,
        target_rows,
        target_rows,
        live_target,
        True,
        slot_size,
    )
    grad_target = grad_first + grad_self_query + grad_self_source
    return (
        grad_target,
        grad_encoded,
        (
            self_grads,
            cross_grads,
            grad_up,
            grad_down,
            (gain_three, gain_four, gain_five),
            (shift_three, shift_four, shift_five),
        ),
    )


def body(
    source,
    target,
    cotangent,
    short_lengths,
    long_lengths,
    attn_weights,
    up_weights,
    down_weights,
    norm_gains,
    norm_shifts,
):
    decoded_all, grad_sources, grad_targets, per_batch = ([], [], [], [])
    for batch_index, slot_size, lengths in ((0, SHORT, short_lengths), (1, LONG, long_lengths)):
        live_source = live_mask(lengths[0], slot_size)
        live_target = live_mask(lengths[1], slot_size)
        source_rows = source[batch_index]
        target_rows = target[batch_index]
        cot_rows = cotangent[batch_index].astype(jnp.float32)
        encoded, enc_saved = encoder_forward(
            source_rows,
            attn_weights,
            up_weights,
            down_weights,
            norm_gains,
            norm_shifts,
            live_source,
            slot_size,
        )
        encoded_low = encoded.astype(jnp.bfloat16)
        decoded, dec_saved = decoder_forward(
            target_rows,
            encoded_low,
            attn_weights,
            up_weights,
            down_weights,
            norm_gains,
            norm_shifts,
            live_source,
            live_target,
            slot_size,
        )
        decoded_all.append(decoded.astype(jnp.bfloat16))
        target_again, encoded_again, cot_rows = lax.optimization_barrier(
            (target_rows, encoded_low, cot_rows)
        )
        unused, dec_saved = decoder_forward(
            target_again,
            encoded_again,
            attn_weights,
            up_weights,
            down_weights,
            norm_gains,
            norm_shifts,
            live_source,
            live_target,
            slot_size,
        )
        grad_target, grad_encoded, dec_grads = decoder_backward(
            dec_saved,
            cot_rows,
            attn_weights,
            up_weights,
            down_weights,
            norm_gains,
            norm_shifts,
            live_source,
            live_target,
            slot_size,
        )
        source_again, grad_encoded = lax.optimization_barrier((source_rows, grad_encoded))
        unused, enc_saved = encoder_forward(
            source_again,
            attn_weights,
            up_weights,
            down_weights,
            norm_gains,
            norm_shifts,
            live_source,
            slot_size,
        )
        grad_source, enc_grads = encoder_backward(
            enc_saved,
            grad_encoded,
            attn_weights,
            up_weights,
            down_weights,
            norm_gains,
            norm_shifts,
            live_source,
            slot_size,
        )
        grad_sources.append(grad_source)
        grad_targets.append(grad_target)
        attn_part = jnp.concatenate([enc_grads[0], dec_grads[0], dec_grads[1]], axis=0)
        up_part = jnp.stack([enc_grads[1], dec_grads[2]])
        down_part = jnp.stack([enc_grads[2], dec_grads[3]])
        gain_part = jnp.stack(
            [enc_grads[3][0], enc_grads[3][1], dec_grads[4][0], dec_grads[4][1], dec_grads[4][2]]
        )
        shift_part = jnp.stack(
            [enc_grads[4][0], enc_grads[4][1], dec_grads[5][0], dec_grads[5][1], dec_grads[5][2]]
        )
        grads = (attn_part, up_part, down_part, gain_part, shift_part)
        per_batch.append(grads)
    summed = tuple(
        (first_part + second_part for first_part, second_part in zip(per_batch[0], per_batch[1]))
    )
    summed = (
        lax.psum_scatter(summed[0], ("dp", "head"), scatter_dimension=1, tiled=True),
        lax.psum_scatter(summed[1], ("dp", "head"), scatter_dimension=1, tiled=True),
        lax.psum_scatter(summed[2], ("dp", "head"), scatter_dimension=1, tiled=True),
        lax.psum_scatter(summed[3], ("dp", "head"), scatter_dimension=1, tiled=True),
        lax.psum_scatter(summed[4], ("dp", "head"), scatter_dimension=1, tiled=True),
    )
    return (
        jnp.stack(decoded_all),
        jnp.stack(grad_sources),
        jnp.stack(grad_targets),
        summed[0],
        summed[1],
        summed[2],
        summed[3],
        summed[4],
    )


def solution(mesh):
    return jax.shard_map(
        body,
        mesh=mesh,
        in_specs=(
            P(None, ("dp", "head"), None),
            P(None, ("dp", "head"), None),
            P(None, ("dp", "head"), None),
            P(None, "dp"),
            P(None, "dp"),
            P(),
            P(),
            P(),
            P(),
            P(),
        ),
        out_specs=(
            P(None, ("dp", "head"), None),
            P(None, ("dp", "head"), None),
            P(None, ("dp", "head"), None),
            P(None, ("dp", "head"), None),
            P(None, ("dp", "head"), None),
            P(None, ("dp", "head"), None),
            P(None, ("dp", "head")),
            P(None, ("dp", "head")),
        ),
        check_vma=False,
    )
```

profile of v0, /device:TPU:0, one launch (start us, length us, event | category | flops | bytes accessed | tf_op | source)
XLA Modules:
  0.0 1832.6 jit_solution(17320393975157527741)
XLA Ops:
  53.2 6.5 all-to-all-done.4
  81.7 5.7 all-to-all-done.6
  94.0 5.7 all-to-all-done.2
  106.9 5.8 all-to-all-done
  118.8 6.3 all-to-all-done.1
  141.9 23.1 %while.220 = (s32[]{:T(128)}, bf16[2,1024,1,2,64]{1,4,3,2,0:T(8,128)(2,1)S(1)}, bf16[2,1024,2,64]{1,3,2,0:T(8,128)(2,1)S(1)}, pred[2,1024]{1,0:T(4,128)(4,1)S(1)...) while((s32[]{:T(128)}, ...), condition=%wide.region_31.32_spmd, body=%wide.region_28.31_spmd.sunk | while | flops 549585920 | bytes 17847376 | solution.py:102
  141.9 7.3 fusion.1246
  153.5 7.2 fusion.1246
  175.0 10.8 while.216
  210.7 25.9 %while.219 = (s32[]{:T(128)}, bf16[2,1024,1,2,64]{1,4,3,2,0:T(8,128)(2,1)}, bf16[2,1024,2,64]{1,3,2,0:T(8,128)(2,1)}, pred[2,1024]{1,0:T(4,128)(4,1)S(1)}, bf16[...) while((s32[]{:T(128)}, bf16[2,1024,1,2,64]{1,4,3,2,0:T(8,128)(2,1)}, ...), condition=%wide.region_25.26_spmd, body=%wide.region_22.25_spmd.sunk | while | flops 551683072 | bytes 19944528 | solution.py:102
  211.1 7.5 fusion.1241
  218.6 5.0 fusion.1242
  224.1 7.5 fusion.1241
  231.6 5.0 fusion.1242
  237.5 12.0 while.217
  267.5 5.2 fusion.954
  281.7 5.2 fusion.948
  307.4 6.6 all-to-all-done.8
  333.7 6.6 all-to-all-done.9
  346.9 6.4 all-to-all-done.20
  360.0 6.4 all-to-all-done.22
  384.5 6.5 all-to-all-done.44
  397.4 6.6 all-to-all-done.45
  411.7 5.3 all-to-all-done.46
  424.0 5.4 all-to-all-done.49
  435.1 6.5 all-to-all-done.25
  471.5 14.3 while.227
  506.2 14.7 while.222
  530.5 10.3 while.218
  552.5 23.1 %while.221 = (s32[]{:T(128)}, bf16[2,1024,1,2,64]{1,4,3,2,0:T(8,128)(2,1)S(1)}, bf16[2,1024,2,64]{1,3,2,0:T(8,128)(2,1)S(1)}, pred[2,1024]{1,0:T(4,128)(4,1)S(1)...) while((s32[]{:T(128)}, ...), condition=%wide.region_39.40_spmd, body=%wide.region_36.39_spmd.sunk | while | flops 549585920 | bytes 17847376 | solution.py:102
  552.5 7.3 fusion.1251
  564.1 7.2 fusion.1251
  598.9 5.7 fusion.974
  616.3 5.7 fusion.967
  656.8 12.5 while.228
  679.3 17.7 while.223
  761.3 6.6 all-to-all-done.51
  780.1 25.7 %while.229 = (s32[]{:T(128)}, bf16[2,1024,1,2,64]{1,4,3,2,0:T(8,128)(2,1)S(1)}, bf16[2,1024,1,2,64]{1,4,3,2,0:T(8,128)(2,1)S(1)}, bf16[2,1024,1,2,64]{1,4,3,2,0:...) while((s32[]{:T(128)}, ...), condition=%wide.region_100.101_spmd, body=%wide.region_98.100_spmd.sunk | while | flops 1374287872 | bytes 73992424 | solution.py:176
  811.9 5.9 convolution_bitcast_fusion.2
  829.6 26.5 %while.224 = (s32[]{:T(128)}, bf16[2,1024,1,2,64]{1,4,3,2,0:T(8,128)(2,1)}, bf16[2,1024,1,2,64]{1,4,3,2,0:T(8,128)(2,1)}, bf16[2,1024,1,2,64]{1,4,3,2,0:T(8,128)...) while((s32[]{:T(128)}, ...), condition=%wide.region_64.65_spmd, body=%wide.region_62.64_spmd.sunk | while | flops 340916224 | bytes 48281476 | solution.py:176
  951.6 4.6 all-to-all-done.55
  962.1 6.4 all-to-all-done.56
  975.8 5.8 all-to-all-done.35
  987.4 6.5 all-to-all-done.36
  1010.8 12.5 while.230
  1039.9 11.5 while.225
  1104.3 5.7 convolution_bitcast_fusion.1
  1111.0 9.8 maximum_add_fusion.1
  1122.6 25.8 %while.233 = (s32[]{:T(128)}, bf16[2,1024,1,2,64]{1,4,3,2,0:T(8,128)(2,1)S(1)}, bf16[2,1024,1,2,64]{1,4,3,2,0:T(8,128)(2,1)S(1)}, bf16[2,1024,1,2,64]{1,4,3,2,0:...) while((s32[]{:T(128)}, ...), condition=%wide.region_125.126_spmd, body=%wide.region_123.125_spmd.sunk | while | flops 1376385024 | bytes 69795952 | solution.py:176
  1154.8 5.1 convolution_bitcast_fusion.4
  1175.0 26.6 %while.232 = (s32[]{:T(128)}, bf16[2,1024,1,2,64]{1,4,3,2,0:T(8,128)(2,1)}, bf16[2,1024,1,2,64]{1,4,3,2,0:T(8,128)(2,1)}, bf16[2,1024,1,2,64]{1,4,3,2,0:T(8,128)...) while((s32[]{:T(128)}, ...), condition=%wide.region_120.121_spmd, body=%wide.region_118.120_spmd.sunk | while | flops 341243904 | bytes 48936836 | solution.py:176
  1224.7 5.9 all-to-all-done.71
  1234.9 4.9 convolution_bitcast_fusion.5
  1249.5 4.9 convolution_bitcast_fusion.7
  1259.7 9.7 maximum_add_fusion
  1289.5 25.5 %while.231 = (s32[]{:T(128)}, bf16[2,1024,1,2,64]{1,4,3,2,0:T(8,128)(2,1)}, bf16[2,1024,1,2,64]{1,4,3,2,0:T(8,128)(2,1)}, bf16[2,1024,1,2,64]{1,4,3,2,0:T(8,128)...) while((s32[]{:T(128)}, ...), condition=%wide.region_115.116_spmd, body=%wide.region_113.115_spmd.sunk | while | flops 1374287872 | bytes 73992416 | solution.py:176
  1324.8 6.7 all-to-all-done.59
  1351.0 26.5 %while.226 = (s32[]{:T(128)}, bf16[2,1024,1,2,64]{1,4,3,2,0:T(8,128)(2,1)}, bf16[2,1024,1,2,64]{1,4,3,2,0:T(8,128)(2,1)}, bf16[2,1024,1,2,64]{1,4,3,2,0:T(8,128)...) while((s32[]{:T(128)}, ...), condition=%wide.region_79.80_spmd, body=%wide.region_77.79_spmd.sunk | while | flops 340916224 | bytes 48281476 | solution.py:176
  1387.3 12.4 all-to-all-done.40
  1405.7 12.6 all-to-all-done.41
  1475.3 6.3 add.700
  1514.4 5.8 reduce-scatter.14.cloned.1.call-done
  1520.1 147.6 %reduce-scatter.12.cloned.1.call-done = f32[2,16,2048]{2,1,0:T(8,128)} async-done(((f32[2,512,2048]{2,1,0:T(8,128)}), f32[2,16,2048]{2,1,0:T(8,128)}) %reduce-scatter.12.cloned.1.call-update) | async-done | bytes 262160 | tf_op jit(solution)/shard_map/reduce_scatter | solution.py:510
  1667.8 158.1 %reduce-scatter.10.cloned.1.call-done = f32[12,16,512]{2,1,0:T(8,128)} async-done(((f32[12,512,512]{2,1,0:T(8,128)}), f32[12,16,512]{2,1,0:T(8,128)}) %reduce-scatter.10.cloned.1.call-update) | async-done | bytes 393232 | tf_op jit(solution)/shard_map/reduce_scatter | solution.py:509
  (1925 shorter events, 1216.0 us)
Async XLA Ops:
  9.7 13.1 all-to-all-start.16
  47.4 12.3 all-to-all-start.4
  59.7 15.4 all-to-all-start.5
  75.1 12.3 all-to-all-start.6
  99.7 13.1 all-to-all-start
  138.1 32.4 %all-to-all-start.13 = ((bf16[512,4,2,64]{0,3,2,1:T(8,128)(2,1)}), bf16[512,4,2,64]{0,3,2,1:T(8,128)(2,1)S(1)}, u32[]{:S(2)}, u32[]{:S(2)}) async-start(bf16[512,4,2,64]{0,3,2,1:T(8,128)(2,1)} %bitcast.1987), calls=%async_computation.13 | async-start | bytes 1048576 | tf_op jit(solution)/shard_map/all_to_all | solution.py:196
  170.5 32.6 %all-to-all-start.14 = ((bf16[512,4,2,64]{0,3,2,1:T(8,128)(2,1)}), bf16[512,4,2,64]{0,3,2,1:T(8,128)(2,1)}, u32[]{:S(2)}, u32[]{:S(2)}) async-start(bf16[512,4,2,64]{0,3,2,1:T(8,128)(2,1)} %bitcast.1985), calls=%async_computation.14 | async-start | bytes 1048576 | tf_op jit(solution)/shard_map/all_to_all | solution.py:197
  203.2 56.5 %all-to-all-start.19 = ((bf16[4,2,32768]{2,1,0:T(2,128)(2,1)}), bf16[4,2,32768]{2,1,0:T(2,128)(2,1)S(1)}, u32[]{:S(2)}, u32[]{:S(2)}) async-start(bf16[4,2,32768]{2,1,0:T(2,128)(2,1)} %reshape.2093), calls=%async_computation.19 | async-start | bytes 1048576 | tf_op jit(solution)/shard_map/all_to_all | solution.py:203
  259.7 13.2 all-to-all-start.7
  273.7 13.4 all-to-all-start.3
  287.8 13.0 all-to-all-start.15
  300.9 13.1 all-to-all-start.8
  313.9 13.2 all-to-all-start.10
  327.2 13.1 all-to-all-start.9
  340.2 13.1 all-to-all-start.20
  353.3 13.1 all-to-all-start.22
  390.9 13.0 all-to-all-start.45
  404.0 13.1 all-to-all-start.46
  453.9 12.8 all-to-all-start.27
  467.6 33.4 %all-to-all-start.43 = ((bf16[512,4,2,64]{0,3,2,1:T(8,128)(2,1)}), bf16[512,4,2,64]{0,3,2,1:T(8,128)(2,1)S(1)}, u32[]{:S(2)}, u32[]{:S(2)}) async-start(bf16[512,4,2,64]{0,3,2,1:T(8,128)(2,1)} %bitcast.1986), calls=%async_computation.43 | async-start | bytes 1048576 | tf_op jit(solution)/shard_map/all_to_all | solution.py:197
  501.0 25.9 %all-to-all-start.30 = ((bf16[512,4,2,64]{0,3,2,1:T(8,128)(2,1)}), bf16[512,4,2,64]{0,3,2,1:T(8,128)(2,1)}, u32[]{:S(2)}, u32[]{:S(2)}) async-start(bf16[512,4,2,64]{0,3,2,1:T(8,128)(2,1)} %bitcast.1984), calls=%async_computation.30 | async-start | bytes 1048576 | tf_op jit(solution)/shard_map/all_to_all | solution.py:198
  526.9 21.7 %all-to-all-start.24 = ((bf16[512,4,2,64]{0,3,2,1:T(8,128)(2,1)}), bf16[512,4,2,64]{0,3,2,1:T(8,128)(2,1)S(1)}, u32[]{:S(2)}, u32[]{:S(2)}) async-start(bf16[512,4,2,64]{0,3,2,1:T(8,128)(2,1)} %bitcast.1983), calls=%async_computation.24 | async-start | bytes 1048576 | tf_op jit(solution)/shard_map/all_to_all | solution.py:197
  548.7 41.6 %all-to-all-start.11 = ((bf16[4,2,32768]{2,1,0:T(2,128)(2,1)}), bf16[4,2,32768]{2,1,0:T(2,128)(2,1)S(1)}, u32[]{:S(2)}, u32[]{:S(2)}) async-start(bf16[4,2,32768]{2,1,0:T(2,128)(2,1)} %reshape.2103), calls=%async_computation.11 | async-start | bytes 1048576 | tf_op jit(solution)/shard_map/all_to_all | solution.py:203
  590.3 15.3 all-to-all-start.23
  605.6 16.7 all-to-all-start.47
  622.3 14.0 all-to-all-start.28
  636.2 14.3 all-to-all-start.48
  650.6 21.0 %all-to-all-start.29 = ((bf16[512,4,2,64]{0,3,2,1:T(8,128)(2,1)}), bf16[512,4,2,64]{0,3,2,1:T(8,128)(2,1)}, u32[]{:S(2)}, u32[]{:S(2)}) async-start(bf16[512,4,2,64]{0,3,2,1:T(8,128)(2,1)} %bitcast.246), calls=%async_computation.29 | async-start | bytes 1048576 | tf_op jit(solution)/shard_map/all_to_all | solution.py:196
  671.6 29.4 %all-to-all-start.50 = ((bf16[4,2,32768]{2,1,0:T(2,128)(2,1)}), bf16[4,2,32768]{2,1,0:T(2,128)(2,1)}, u32[]{:S(2)}, u32[]{:S(2)}) async-start(bf16[4,2,32768]{2,1,0:T(2,128)(2,1)} %reshape.2107), calls=%async_computation.50 | async-start | bytes 1048576 | tf_op jit(solution)/shard_map/all_to_all | solution.py:203
  701.0 17.1 all-to-all-start.31
  754.8 13.1 all-to-all-start.51
  767.9 40.3 %all-to-all-start.32 = ((bf16[512,4,2,64]{0,3,2,1:T(8,128)(2,1)}), bf16[512,4,2,64]{0,3,2,1:T(8,128)(2,1)}, u32[]{:S(2)}, u32[]{:S(2)}) async-start(bf16[512,4,2,64]{0,3,2,1:T(8,128)(2,1)} %bitcast.1907), calls=%async_computation.32 | async-start | bytes 1048576 | tf_op jit(solution)/shard_map/all_to_all | solution.py:217
  808.2 14.7 all-to-all-start.52
  822.9 47.5 %all-to-all-start.53 = ((bf16[4,2,32768]{2,1,0:T(2,128)(2,1)}), bf16[4,2,32768]{2,1,0:T(2,128)(2,1)}, u32[]{:S(2)}, u32[]{:S(2)}) async-start(bf16[4,2,32768]{2,1,0:T(2,128)(2,1)} %reshape.2111), calls=%async_computation.53 | async-start | bytes 1048576 | tf_op jit(solution)/shard_map/all_to_all | solution.py:226
  870.4 13.2 all-to-all-start.33
  883.5 12.7 all-to-all-start.34
  896.2 14.9 all-to-all-start.67
  923.3 19.7 %all-to-all-start.54 = ((bf16[512,4,2,64]{0,3,2,1:T(8,128)(2,1)}), bf16[512,4,2,64]{0,3,2,1:T(8,128)(2,1)}, u32[]{:S(2)}, u32[]{:S(2)}) async-start(bf16[512,4,2,64]{0,3,2,1:T(8,128)(2,1)} %bitcast.1993), calls=%async_computation.54 | async-start | bytes 1048576 | tf_op jit(solution)/shard_map/all_to_all | solution.py:198
  943.0 13.2 all-to-all-start.55
  968.5 13.1 all-to-all-start.35
  993.9 12.4 all-to-all-start.37
  1006.3 28.4 %all-to-all-start.68 = ((bf16[512,4,2,64]{0,3,2,1:T(8,128)(2,1)}), bf16[512,4,2,64]{0,3,2,1:T(8,128)(2,1)}, u32[]{:S(2)}, u32[]{:S(2)}) async-start(bf16[512,4,2,64]{0,3,2,1:T(8,128)(2,1)} %bitcast.393), calls=%async_computation.68 | async-start | bytes 1048576 | tf_op jit(solution)/shard_map/all_to_all | solution.py:217
  1034.7 23.5 %all-to-all-start.57 = ((bf16[4,2,32768]{2,1,0:T(2,128)(2,1)}), bf16[4,2,32768]{2,1,0:T(2,128)(2,1)}, u32[]{:S(2)}, u32[]{:S(2)}) async-start(bf16[4,2,32768]{2,1,0:T(2,128)(2,1)} %reshape.2113), calls=%async_computation.57 | async-start | bytes 1048576 | tf_op jit(solution)/shard_map/all_to_all | solution.py:203
  1058.2 13.8 all-to-all-start.38
  1072.0 78.7 %all-to-all-start.63 = ((bf16[512,4,2,64]{0,3,2,1:T(8,128)(2,1)}), bf16[512,4,2,64]{0,3,2,1:T(8,128)(2,1)}, u32[]{:S(2)}, u32[]{:S(2)}) async-start(bf16[512,4,2,64]{0,3,2,1:T(8,128)(2,1)} %bitcast.372), calls=%async_computation.63 | async-start | bytes 1048576 | tf_op jit(solution)/shard_map/all_to_all | solution.py:217
  1076.1 424.0 %reduce-scatter.18.cloned.1.call-start = ((), (), s32[]{:S(2)}) async-start(), calls=%async_computation.81 | async-start | bytes 270336
  1104.2 397.3 %reduce-scatter.16.cloned.1.call-start = ((), (), s32[]{:S(2)}) async-start(), calls=%async_computation.80 | async-start | bytes 270336
  1111.0 409.2 %reduce-scatter.14.cloned.1.call-start = ((), (), s32[]{:S(2)}) async-start(), calls=%async_computation.79 | async-start | bytes 8650752 | tf_op jit(solution)/shard_map/reduce_scatter | solution.py:511
  1150.7 17.5 all-to-all-start.69
  1168.2 49.1 %all-to-all-start.70 = ((bf16[4,2,32768]{2,1,0:T(2,128)(2,1)}), bf16[4,2,32768]{2,1,0:T(2,128)(2,1)}, u32[]{:S(2)}, u32[]{:S(2)}) async-start(bf16[4,2,32768]{2,1,0:T(2,128)(2,1)} %reshape.2141), calls=%async_computation.70 | async-start | bytes 1048576 | tf_op jit(solution)/shard_map/all_to_all | solution.py:225
  1217.3 13.2 all-to-all-start.71
  1230.5 13.2 all-to-all-start.64
  1243.7 12.4 all-to-all-start.65
  1256.2 13.3 all-to-all-start.58
  1259.6 408.1 %reduce-scatter.12.cloned.1.call-start = ((), (), s32[]{:S(2)}) async-start(), calls=%async_computation.78 | async-start | bytes 8650752 | tf_op jit(solution)/shard_map/reduce_scatter | solution.py:510
  1270.3 12.5 all-to-all-start.66
  1282.7 36.2 %all-to-all-start.39 = ((bf16[512,4,2,64]{0,3,2,1:T(8,128)(2,1)}), bf16[512,4,2,64]{0,3,2,1:T(8,128)(2,1)}, u32[]{:S(2)}, u32[]{:S(2)}) async-start(bf16[512,4,2,64]{0,3,2,1:T(8,128)(2,1)} %bitcast.1906), calls=%async_computation.39 | async-start | bytes 1048576 | tf_op jit(solution)/shard_map/all_to_all | solution.py:217
  1319.0 12.5 all-to-all-start.59
  1331.4 12.3 all-to-all-start.60
  1343.8 37.7 %all-to-all-start.61 = ((bf16[4,2,32768]{2,1,0:T(2,128)(2,1)}), bf16[4,2,32768]{2,1,0:T(2,128)(2,1)}, u32[]{:S(2)}, u32[]{:S(2)}) async-start(bf16[4,2,32768]{2,1,0:T(2,128)(2,1)} %reshape.2119), calls=%async_computation.61 | async-start | bytes 1048576 | tf_op jit(solution)/shard_map/all_to_all | solution.py:226
  1381.5 18.2 all-to-all-start.40
  1399.7 18.6 %all-to-all-start.41 = ((bf16[4,2,32768]{2,1,0:T(2,128)(2,1)}), bf16[4,2,32768]{2,1,0:T(2,128)(2,1)S(1)}, u32[]{:S(2)}, u32[]{:S(2)}) async-start(bf16[4,2,32768]{2,1,0:T(2,128)(2,1)} %reshape.2133), calls=%async_computation.41 | async-start | bytes 1048576 | tf_op jit(solution)/shard_map/all_to_all | solution.py:225
  1418.3 36.9 %all-to-all-start.42 = ((bf16[4,2,32768]{2,1,0:T(2,128)(2,1)}), bf16[4,2,32768]{2,1,0:T(2,128)(2,1)}, u32[]{:S(2)}, u32[]{:S(2)}) async-start(bf16[4,2,32768]{2,1,0:T(2,128)(2,1)} %reshape.2135), calls=%async_computation.42 | async-start | bytes 1048576 | tf_op jit(solution)/shard_map/all_to_all | solution.py:226
  1422.5 403.4 %reduce-scatter.10.cloned.1.call-start = ((), (), s32[]{:S(2)}) async-start(), calls=%async_computation.77 | async-start | bytes 12976128 | tf_op jit(solution)/shard_map/reduce_scatter | solution.py:509
  (422 other events, 4003.9 us)
Sparse Core Ops, SparseCore 0:
  1104.3 135.9 reduce-scatter.17
  1242.6 129.4 reduce-scatter.15
  1375.0 145.1 reduce-scatter.13
  1522.9 144.8 reduce-scatter.11
  1674.2 151.5 reduce-scatter.9
where the time goes:
time: 1850 us; the launch traced here: 1830 us
  waiting for transfers between devices  506 us (27%)
  matrix products  471 us (25%)
  local copies, waits for them, and re-layouts  460 us (25%)
  starting transfers between devices  279 us (15%)
  other arithmetic  93.8 us (5%)
  between operations  20.5 us (1%)
    reduce_scatter x1, waiting for transfers between devices, body(): lax.psum_scatter(summed[0], ('dp', 'head'), scatter_dimension=1, tiled=True)  158 us
    reduce_scatter x1, waiting for transfers between devices, body(): lax.psum_scatter(summed[1], ('dp', 'head'), scatter_dimension=1, tiled=True)  148 us
    dot_general x60, matrix products, matmul(): return jnp.dot(operand, weight, preferred_element_type=jnp.float32)  141 us
    unnamed x749, local copies, waits for them, and re-layouts  130 us
    dot_general x32, matrix products, left_grad(): lax.dot_general(gradient, weight, (((1,), (1,)), ((), ())), preferred_ele...  66.7 us
    dot_general x24, matrix products, one_block(): jnp.einsum('ahqk,akhd->aqhd', softmax_low, value_rows.reshape(slot_shape)...  58.9 us
    sub x12, matrix products, one_block(): powers = jnp.exp(scores - highest)  57 us
    all_to_all x12, waiting for transfers between devices, attention_forward(): lax.all_to_all(split_heads(value_flat), 'head', split_axis=1, concat_axis...  53.8 us
  transfers between devices with their start and end apart: 77, of which 39 were waited for; matrix products, arithmetic and copies ran while one was open for 52% of the time, Pallas kernels for 0%

commit v1 on v0

v1 whole, which is shorter than its diff:
```python
import functools
import math

import jax
import jax.numpy as jnp
from jax import lax
from jax.experimental import pallas as pl
from jax.experimental.pallas import tpu as pltpu
from jax.sharding import PartitionSpec as P

HEADS = 8
SHORT = 256
LONG = 1024

EPSILON = 1e-05
MASKED = -1e30
F32 = jnp.float32
BF16 = jnp.bfloat16
AXES = ("dp", "head")
COLS = 256
CHUNK = 512

NN = (((1,), (0,)), ((), ()))
NT = (((1,), (1,)), ((), ()))
TN = (((0,), (0,)), ((), ()))


def dot(left, right, dims=NN):
    return lax.dot_general(left, right, dims, preferred_element_type=F32)


def params():
    return pltpu.CompilerParams(vmem_limit_bytes=63 << 20)


def cost(flops, moved, powers=0):
    return pl.CostEstimate(flops=int(flops), bytes_accessed=int(moved), transcendentals=int(powers))


def whole(array):
    return pl.BlockSpec(array.shape, lambda *step: (0,) * array.ndim)


def shaped(shape, kind):
    return jax.ShapeDtypeStruct(shape, kind)


def lanes():
    return lax.broadcasted_iota(jnp.int32, (1, 128), 1)


def one_head(which, pair):
    keep = (lanes() < 64) if which == 0 else (lanes() >= 64)
    return jnp.where(keep, pair, jnp.zeros_like(pair))


def join_heads(first, second):
    return jnp.where(lanes() < 64, first, second)


def scores_bias(bias_ref, slot, width, causal):
    bias = bias_ref[slot : slot + 1, :]
    if not causal:
        return bias
    keys = bias.shape[1]
    row = lax.broadcasted_iota(jnp.int32, (width, width), 0)
    column = lax.broadcasted_iota(jnp.int32, (width, width), 1)
    own = jnp.where(column <= row, bias[:, :width], MASKED)
    if keys == width:
        return own
    rest = jnp.broadcast_to(bias[:, width:], (width, keys - width))
    return jnp.concatenate([own, rest], axis=1)


def attend_rows(bias, q_ref, k_ref, v_ref, e_ref, o_ref, inv_ref, rows, keys):
    count = bias.shape[1]
    ones = jnp.ones((count, 128), BF16)
    for pair in range(COLS // 128):
        cols = slice(pair * 128, pair * 128 + 128)
        queries = q_ref[rows, cols]
        key_pair = k_ref[keys, cols]
        value_ext = jnp.concatenate([v_ref[keys, cols], ones], axis=1)
        outs, inverses = [], []
        for which in range(2):
            scores = dot(one_head(which, queries), key_pair, NT) + bias
            highest = jnp.max(scores, axis=1, keepdims=True)
            powers = jnp.exp(scores - highest).astype(BF16)
            e_ref[pair * 2 + which, rows, :] = powers
            mixed = dot(powers, value_ext)
            inverse = 1.0 / mixed[:, 128:]
            outs.append(mixed[:, :128] * inverse)
            inverses.append(inverse)
        o_ref[rows, cols] = join_heads(*outs).astype(BF16)
        inv_ref[rows, cols] = join_heads(*inverses)


def attend_kernel(causal, self_keys, *refs):
    xq_ref, *rest = refs
    xk_ref = xq_ref if self_keys else rest.pop(0)
    (
        mate_ref,
        wq_ref,
        wk_ref,
        wv_ref,
        bias_s_ref,
        bias_l_ref,
        o_ref,
        inv_ref,
        q_ref,
        ks_ref,
        vs_ref,
        kl_ref,
        vl_ref,
        es_ref,
        el_ref,
    ) = rest
    rows = xq_ref.shape[1]
    scale = 0.125
    for batch in range(2):
        q_ref[batch] = (dot(xq_ref[batch], wq_ref[0]) * scale).astype(BF16)
    ks_ref[...] = dot(xk_ref[0], wk_ref[0]).astype(BF16)
    vs_ref[...] = dot(xk_ref[0], wv_ref[0]).astype(BF16)
    kl_ref[:rows] = dot(xk_ref[1], wk_ref[0]).astype(BF16)
    vl_ref[:rows] = dot(xk_ref[1], wv_ref[0]).astype(BF16)
    kl_ref[rows:] = dot(mate_ref[...], wk_ref[0]).astype(BF16)
    vl_ref[rows:] = dot(mate_ref[...], wv_ref[0]).astype(BF16)
    everything = slice(None)
    bias = scores_bias(bias_l_ref, 0, rows, causal)
    attend_rows(
        bias, q_ref.at[1], kl_ref, vl_ref, el_ref, o_ref.at[1], inv_ref.at[1], everything, everything
    )
    for slot in range(rows // SHORT):
        bias = scores_bias(bias_s_ref, slot, SHORT, causal)
        here = slice(slot * SHORT, (slot + 1) * SHORT)
        attend_rows(
            bias, q_ref.at[0], ks_ref, vs_ref, es_ref, o_ref.at[0], inv_ref.at[0], here, here
        )


def attend(queries, keys, mate, weights, base, bias_s, bias_l, causal):
    _, rows, width = queries.shape
    self_keys = keys is None
    heads = width // 64
    weight = lambda index: pl.BlockSpec((1, width, COLS), lambda step: (index, 0, step))
    both = pl.BlockSpec((2, rows, COLS), lambda step: (0, 0, step))
    cols = lambda count: pl.BlockSpec((count, COLS), lambda step: (0, step))
    powers = lambda count: pl.BlockSpec((COLS // 64, rows, count), lambda step: (step, 0, 0))
    xs = (queries,) if self_keys else (queries, keys)
    flops = 2 * rows * width * width * 7 + 4 * rows * width * (SHORT + LONG)
    return pl.pallas_call(
        functools.partial(attend_kernel, causal, self_keys),
        grid=(width // COLS,),
        out_shape=(
            shaped((2, rows, width), BF16),
            shaped((2, rows, width), F32),
            shaped((2, rows, width), BF16),
            shaped((rows, width), BF16),
            shaped((rows, width), BF16),
            shaped((LONG, width), BF16),
            shaped((LONG, width), BF16),
            shaped((heads, rows, SHORT), BF16),
            shaped((heads, rows, LONG), BF16),
        ),
        in_specs=[whole(x) for x in xs]
        + [whole(mate)]
        + [weight(base), weight(base + 1), weight(base + 2)]
        + [whole(bias_s), whole(bias_l)],
        out_specs=(
            both,
            both,
            both,
            cols(rows),
            cols(rows),
            cols(LONG),
            cols(LONG),
            powers(SHORT),
            powers(LONG),
        ),
        compiler_params=params(),
        cost_estimate=cost(flops * 2, 22 << 20, heads * rows * (SHORT + LONG)),
        name="attend",
    )(*xs, mate, weights, weights, weights, bias_s, bias_l)


def attend_back_rows(
    do_ref, o_ref, inv_ref, q_ref, k_ref, v_ref, e_ref, dq_ref, dk_ref, dv_ref, rows, keys, scale
):
    for pair in range(COLS // 128):
        cols = slice(pair * 128, pair * 128 + 128)
        grad = do_ref[rows, cols].astype(F32) * inv_ref[rows, cols]
        product = grad * o_ref[rows, cols].astype(F32)
        grad_low = grad.astype(BF16)
        queries = q_ref[rows, cols]
        key_pair = k_ref[keys, cols]
        value_pair = v_ref[keys, cols]
        grad_turned = grad.T.astype(BF16)
        queries_turned = queries.astype(F32).T.astype(BF16)
        grad_q, grad_k, grad_v = [], [], []
        for which in range(2):
            inner = jnp.sum(one_head(which, product), axis=1, keepdims=True)
            grad_probs = dot(one_head(which, grad_low), value_pair, NT)
            powers = e_ref[pair * 2 + which, rows, :]
            grad_scores = (powers.astype(F32) * (grad_probs - inner)).astype(BF16)
            grad_q.append(dot(grad_scores, key_pair))
            head = slice(which * 64, which * 64 + 64)
            grad_v.append(dot(grad_turned[head], powers))
            grad_k.append(dot(queries_turned[head], grad_scores))
        dq_ref[rows, cols] = (join_heads(*grad_q) * scale).astype(BF16)
        dk_ref[keys, cols] = jnp.concatenate(grad_k, axis=0).T.astype(BF16)
        dv_ref[keys, cols] = jnp.concatenate(grad_v, axis=0).T.astype(BF16)


def attend_back_kernel(self_keys, *refs):
    (
        do_ref,
        o_ref,
        inv_ref,
        q_ref,
        ks_ref,
        vs_ref,
        kl_ref,
        vl_ref,
        es_ref,
        el_ref,
        resid_ref,
        xq_ref,
        *rest,
    ) = refs
    xk_ref = xq_ref if self_keys else rest.pop(0)
    mate_ref, wq_ref, wk_ref, wv_ref, *rest = rest
    dx_ref = rest.pop(0)
    dy_ref = dx_ref if self_keys else rest.pop(0)
    dmate_ref, dwq_ref, dwk_ref, dwv_ref, dqs, dks, dvs, dql, dkl, dvl, mate_sum = rest
    rows = xq_ref.shape[1]
    scale = 0.125
    everything = slice(None)
    attend_back_rows(
        do_ref.at[1],
        o_ref.at[1],
        inv_ref.at[1],
        q_ref.at[1],
        kl_ref,
        vl_ref,
        el_ref,
        dql,
        dkl,
        dvl,
        everything,
        everything,
        scale,
    )
    for slot in range(rows // SHORT):
        here = slice(slot * SHORT, (slot + 1) * SHORT)
        attend_back_rows(
            do_ref.at[0],
            o_ref.at[0],
            inv_ref.at[0],
            q_ref.at[0],
            ks_ref,
            vs_ref,
            es_ref,
            dqs,
            dks,
            dvs,
            here,
            here,
            scale,
        )
    wq, wk, wv = wq_ref[0], wk_ref[0], wv_ref[0]

    @pl.when(pl.program_id(0) == 0)
    def _():
        dx_ref[...] = resid_ref[...]
        if not self_keys:
            dy_ref[...] = jnp.zeros_like(dy_ref)
        mate_sum[...] = jnp.zeros_like(mate_sum)

    own = slice(0, rows)
    other = slice(rows, 2 * rows)
    dx_ref[0] += dot(dqs[...], wq, NT)
    dx_ref[1] += dot(dql[...], wq, NT)
    dy_ref[0] += dot(dks[...], wk, NT) + dot(dvs[...], wv, NT)
    dy_ref[1] += dot(dkl[own], wk, NT) + dot(dvl[own], wv, NT)
    mate_sum[...] += dot(dkl[other], wk, NT) + dot(dvl[other], wv, NT)
    dwq_ref[...] = (dot(xq_ref[0], dqs[...], TN) + dot(xq_ref[1], dql[...], TN)).astype(BF16)
    short, long, mate = xk_ref[0], xk_ref[1], mate_ref[...]
    dwk_ref[...] = (
        dot(short, dks[...], TN) + dot(long, dkl[own], TN) + dot(mate, dkl[other], TN)
    ).astype(BF16)
    dwv_ref[...] = (
        dot(short, dvs[...], TN) + dot(long, dvl[own], TN) + dot(mate, dvl[other], TN)
    ).astype(BF16)

    @pl.when(pl.program_id(0) == pl.num_programs(0) - 1)
    def _():
        dmate_ref[...] = mate_sum[...].astype(BF16)


def attend_back(grad, saved, resid, queries, keys, mate, weights, base):
    o, inverse, q, ks, vs, kl, vl, es, el = saved
    _, rows, width = queries.shape
    self_keys = keys is None
    heads = width // 64
    weight = lambda index: pl.BlockSpec((1, width, COLS), lambda step: (index, 0, step))
    both = pl.BlockSpec((2, rows, COLS), lambda step: (0, 0, step))
    cols = lambda count: pl.BlockSpec((count, COLS), lambda step: (0, step))
    powers = lambda count: pl.BlockSpec((COLS // 64, rows, count), lambda step: (step, 0, 0))
    full = pl.BlockSpec((2, rows, width), lambda step: (0, 0, 0))
    xs = (queries,) if self_keys else (queries, keys)
    flops = 2 * rows * width * width * 14 + 8 * rows * width * (SHORT + LONG)
    data = (shaped((2, rows, width), F32),) * len(xs)
    return pl.pallas_call(
        functools.partial(attend_back_kernel, self_keys),
        grid=(width // COLS,),
        out_shape=data + (shaped((rows, width), BF16),) + (shaped((width, width), BF16),) * 3,
        in_specs=[both] * 4
        + [cols(rows)] * 2
        + [cols(LONG)] * 2
        + [powers(SHORT), powers(LONG), whole(resid)]
        + [whole(x) for x in xs]
        + [whole(mate), weight(base), weight(base + 1), weight(base + 2)],
        out_specs=(full,) * len(xs)
        + (pl.BlockSpec((rows, width), lambda step: (0, 0)),)
        + (cols(width),) * 3,
        scratch_shapes=[pltpu.VMEM((rows, COLS), BF16)] * 4
        + [pltpu.VMEM((LONG, COLS), BF16)] * 2
        + [pltpu.VMEM((rows, width), F32)],
        compiler_params=params(),
        cost_estimate=cost(flops * 2, 28 << 20),
        name="attend_back",
    )(grad, o, inverse, q, ks, vs, kl, vl, es, el, resid, *xs, mate, weights, weights, weights)


def norm_parts(resid):
    average = jnp.mean(resid, axis=-1, keepdims=True)
    centered = resid - average
    variance = jnp.mean(centered * centered, axis=-1, keepdims=True)
    spread = lax.rsqrt(variance + EPSILON)
    return centered * spread, spread


def norm_back(normal, spread, gain, grad):
    scaled = grad * gain
    first = jnp.mean(scaled, axis=-1, keepdims=True)
    second = jnp.mean(scaled * normal, axis=-1, keepdims=True)
    return (scaled - first - normal * second) * spread


def add_norm_grads(ref, place, grad, normal):
    ref[place : place + 1, :] += jnp.sum(grad * normal, axis=0, keepdims=True)
    ref[place + 1 : place + 2, :] += jnp.sum(grad, axis=0, keepdims=True)


def logistic(value):
    return 1.0 / (1.0 + jnp.exp(-value))


def feed_kernel(chunks, o_ref, x_ref, wo_ref, up_ref, down_ref, gain_ref, shift_ref, r1_ref, u_ref, r2_ref, enc_ref):
    resid = x_ref[0].astype(F32) + dot(o_ref[0], wo_ref[0])
    r1_ref[0] = resid
    normal, _ = norm_parts(resid)
    hidden = normal * gain_ref[0:1] + shift_ref[0:1]
    hidden_low = hidden.astype(BF16)
    total = hidden
    for chunk in range(chunks):
        part = slice(chunk * CHUNK, (chunk + 1) * CHUNK)
        upward = dot(hidden_low, up_ref[0, :, part])
        u_ref[0, :, part] = upward
        active = (upward * logistic(upward)).astype(BF16)
        total = total + dot(active, down_ref[0, part, :])
    r2_ref[0] = total
    normal, _ = norm_parts(total)
    enc_ref[0] = (normal * gain_ref[1:2] + shift_ref[1:2]).astype(BF16)


def feed(o, x, attn, ups, downs, gains, shifts):
    _, rows, width = x.shape
    inner = ups.shape[2]
    row = lambda count: pl.BlockSpec((1, rows, count), lambda batch: (batch, 0, 0))
    pick = lambda array, index: pl.BlockSpec((1,) + array.shape[1:], lambda batch: (index, 0, 0))
    return pl.pallas_call(
        functools.partial(feed_kernel, inner // CHUNK),
        grid=(2,),
        out_shape=(
            shaped((2, rows, width), F32),
            shaped((2, rows, inner), F32),
            shaped((2, rows, width), F32),
            shaped((2, rows, width), BF16),
        ),
        in_specs=[row(width), row(width), pick(attn, 3), pick(ups, 0), pick(downs, 0), whole(gains), whole(shifts)],
        out_specs=(row(width), row(inner), row(width), row(width)),
        compiler_params=params(),
        cost_estimate=cost(4 * rows * width * (width + 2 * inner), 22 << 20, 2 * rows * inner),
        name="feed",
    )(o, x, attn, ups, downs, gains, shifts)


def middle_kernel(o_ref, x_ref, wo_ref, gain_ref, shift_ref, r_ref, low_ref):
    resid = x_ref[0].astype(F32) + dot(o_ref[0], wo_ref[0])
    r_ref[0] = resid
    normal, _ = norm_parts(resid)
    low_ref[0] = (normal * gain_ref[2:3] + shift_ref[2:3]).astype(BF16)


def middle(o, x, attn, gains, shifts):
    _, rows, width = x.shape
    row = lambda count: pl.BlockSpec((1, rows, count), lambda batch: (batch, 0, 0))
    pick = lambda array, index: pl.BlockSpec((1,) + array.shape[1:], lambda batch: (index, 0, 0))
    return pl.pallas_call(
        middle_kernel,
        grid=(2,),
        out_shape=(shaped((2, rows, width), F32), shaped((2, rows, width), BF16)),
        in_specs=[row(width), row(width), pick(attn, 7), whole(gains), whole(shifts)],
        out_specs=(row(width), row(width)),
        compiler_params=params(),
        cost_estimate=cost(4 * rows * width * width, 7 << 20),
        name="middle",
    )(o, x, attn, gains, shifts)


def feed_back_chunks(
    chunks, grad, low, hidden_low, u_ref, a_ref, up_ref, down_ref, up_sum, down_sum
):
    total = grad
    for chunk in range(chunks):
        part = slice(chunk * CHUNK, (chunk + 1) * CHUNK)
        upward = u_ref[:, part]
        gate = logistic(upward)
        if a_ref is None:
            active = (upward * gate).astype(BF16)
        else:
            active = a_ref[:, part]
        grad_active = dot(low, down_ref[0, part, :], NT)
        grad_up = (grad_active * gate * (1.0 + upward * (1.0 - gate))).astype(BF16)
        down_sum[part, :] += dot(active, low, TN)
        up_sum[:, part] += dot(hidden_low, grad_up, TN)
        total = total + dot(grad_up, up_ref[0, :, part], NT)
    return total


def clear_first(*refs):
    @pl.when(pl.program_id(0) == 0)
    def _():
        for ref in refs:
            ref[...] = jnp.zeros_like(ref)


def write_last(*pairs):
    @pl.when(pl.program_id(0) == pl.num_programs(0) - 1)
    def _():
        for ref, total in pairs:
            ref[...] = total[...].astype(BF16)


def turn_kernel(
    chunks,
    o_ref,
    r3_ref,
    cot_ref,
    wo_ref,
    up_ref,
    down_ref,
    gain_ref,
    shift_ref,
    out_ref,
    dr_ref,
    do_ref,
    dup_ref,
    ddown_ref,
    dwo_ref,
    norm_ref,
    u_s,
    a_s,
    up_sum,
    down_sum,
    wo_sum,
):
    clear_first(up_sum, down_sum, wo_sum, norm_ref)
    mixed = o_ref[0]
    normal3, _ = norm_parts(r3_ref[0])
    resid4 = normal3 * gain_ref[2:3] + shift_ref[2:3] + dot(mixed, wo_ref[0])
    normal4, spread4 = norm_parts(resid4)
    hidden = normal4 * gain_ref[3:4] + shift_ref[3:4]
    hidden_low = hidden.astype(BF16)
    total = hidden
    for chunk in range(chunks):
        part = slice(chunk * CHUNK, (chunk + 1) * CHUNK)
        upward = dot(hidden_low, up_ref[0, :, part])
        u_s[:, part] = upward
        active = (upward * logistic(upward)).astype(BF16)
        a_s[:, part] = active
        total = total + dot(active, down_ref[0, part, :])
    normal5, spread5 = norm_parts(total)
    out_ref[0] = (normal5 * gain_ref[4:5] + shift_ref[4:5]).astype(BF16)
    grad = cot_ref[0].astype(F32)
    add_norm_grads(norm_ref, 0, grad, normal5)
    grad = norm_back(normal5, spread5, gain_ref[4:5], grad)
    grad = feed_back_chunks(
        chunks, grad, grad.astype(BF16), hidden_low, u_s, a_s, up_ref, down_ref, up_sum, down_sum
    )
    add_norm_grads(norm_ref, 2, grad, normal4)
    grad = norm_back(normal4, spread4, gain_ref[3:4], grad)
    dr_ref[0] = grad
    low = grad.astype(BF16)
    wo_sum[...] += dot(mixed, low, TN)
    do_ref[0] = dot(low, wo_ref[0], NT).astype(BF16)
    write_last((dup_ref, up_sum), (ddown_ref, down_sum), (dwo_ref, wo_sum))


def turn(o, r3, cot, attn, ups, downs, gains, shifts):
    _, rows, width = r3.shape
    inner = ups.shape[2]
    row = pl.BlockSpec((1, rows, width), lambda batch: (batch, 0, 0))
    pick = lambda array, index: pl.BlockSpec((1,) + array.shape[1:], lambda batch: (index, 0, 0))
    still = lambda *shape: pl.BlockSpec(shape, lambda batch: (0,) * len(shape))
    return pl.pallas_call(
        functools.partial(turn_kernel, inner // CHUNK),
        grid=(2,),
        out_shape=(
            shaped((2, rows, width), BF16),
            shaped((2, rows, width), F32),
            shaped((2, rows, width), BF16),
            shaped((width, inner), BF16),
            shaped((inner, width), BF16),
            shaped((width, width), BF16),
            shaped((8, width), F32),
        ),
        in_specs=[row, row, row, pick(attn, 11), pick(ups, 1), pick(downs, 1), whole(gains), whole(shifts)],
        out_specs=(row, row, row, still(width, inner), still(inner, width), still(width, width), still(8, width)),
        scratch_shapes=[
            pltpu.VMEM((rows, inner), F32),
            pltpu.VMEM((rows, inner), BF16),
            pltpu.VMEM((width, inner), F32),
            pltpu.VMEM((inner, width), F32),
            pltpu.VMEM((width, width), F32),
        ],
        compiler_params=params(),
        cost_estimate=cost(12 * rows * width * (width + 2 * inner), 20 << 20, 4 * rows * inner),
        name="turn",
    )(o, r3, cot, attn, ups, downs, gains, shifts)


def feed_back_kernel(
    chunks,
    grad_ref,
    mate_ref,
    r2_ref,
    r1_ref,
    u_ref,
    o_ref,
    wo_ref,
    up_ref,
    down_ref,
    gain_ref,
    shift_ref,
    dr_ref,
    do_ref,
    dup_ref,
    ddown_ref,
    dwo_ref,
    norm_ref,
    grad_s,
    up_sum,
    down_sum,
    wo_sum,
):
    clear_first(up_sum, down_sum, wo_sum, norm_ref)
    grad_s[...] = grad_ref[0]

    @pl.when(pl.program_id(0) == 1)
    def _():
        grad_s[...] += mate_ref[...].astype(F32)

    grad = grad_s[...]
    normal2, spread2 = norm_parts(r2_ref[0])
    add_norm_grads(norm_ref, 2, grad, normal2)
    grad = norm_back(normal2, spread2, gain_ref[1:2], grad)
    normal1, spread1 = norm_parts(r1_ref[0])
    hidden_low = (normal1 * gain_ref[0:1] + shift_ref[0:1]).astype(BF16)
    grad = feed_back_chunks(
        chunks,
        grad,
        grad.astype(BF16),
        hidden_low,
        u_ref.at[0],
        None,
        up_ref,
        down_ref,
        up_sum,
        down_sum,
    )
    add_norm_grads(norm_ref, 0, grad, normal1)
    grad = norm_back(normal1, spread1, gain_ref[0:1], grad)
    dr_ref[0] = grad
    low = grad.astype(BF16)
    wo_sum[...] += dot(o_ref[0], low, TN)
    do_ref[0] = dot(low, wo_ref[0], NT).astype(BF16)
    write_last((dup_ref, up_sum), (ddown_ref, down_sum), (dwo_ref, wo_sum))


def feed_back(grad, mate, r2, r1, u, o, attn, ups, downs, gains, shifts):
    _, rows, width = r1.shape
    inner = ups.shape[2]
    row = lambda count: pl.BlockSpec((1, rows, count), lambda batch: (batch, 0, 0))
    pick = lambda array, index: pl.BlockSpec((1,) + array.shape[1:], lambda batch: (index, 0, 0))
    still = lambda *shape: pl.BlockSpec(shape, lambda batch: (0,) * len(shape))
    return pl.pallas_call(
        functools.partial(feed_back_kernel, inner // CHUNK),
        grid=(2,),
        out_shape=(
            shaped((2, rows, width), F32),
            shaped((2, rows, width), BF16),
            shaped((width, inner), BF16),
            shaped((inner, width), BF16),
            shaped((width, width), BF16),
            shaped((8, width), F32),
        ),
        in_specs=[
            row(width),
            whole(mate),
            row(width),
            row(width),
            row(inner),
            row(width),
            pick(attn, 3),
            pick(ups, 0),
            pick(downs, 0),
            whole(gains),
            whole(shifts),
        ],
        out_specs=(row(width), row(width), still(width, inner), still(inner, width), still(width, width), still(8, width)),
        scratch_shapes=[
            pltpu.VMEM((rows, width), F32),
            pltpu.VMEM((width, inner), F32),
            pltpu.VMEM((inner, width), F32),
            pltpu.VMEM((width, width), F32),
        ],
        compiler_params=params(),
        cost_estimate=cost(8 * rows * width * (width + 2 * inner), 30 << 20, 2 * rows * inner),
        name="feed_back",
    )(grad, mate, r2, r1, u, o, attn, ups, downs, gains, shifts)


def middle_back_kernel(grad_ref, r_ref, o_ref, wo_ref, gain_ref, dr_ref, do_ref, dwo_ref, norm_ref, wo_sum):
    clear_first(wo_sum, norm_ref)
    grad = grad_ref[0]
    normal, spread = norm_parts(r_ref[0])
    add_norm_grads(norm_ref, 0, grad, normal)
    grad = norm_back(normal, spread, gain_ref[2:3], grad)
    dr_ref[0] = grad
    low = grad.astype(BF16)
    wo_sum[...] += dot(o_ref[0], low, TN)
    do_ref[0] = dot(low, wo_ref[0], NT).astype(BF16)
    write_last((dwo_ref, wo_sum))


def middle_back(grad, r, o, attn, gains):
    _, rows, width = r.shape
    row = pl.BlockSpec((1, rows, width), lambda batch: (batch, 0, 0))
    pick = lambda array, index: pl.BlockSpec((1,) + array.shape[1:], lambda batch: (index, 0, 0))
    still = lambda *shape: pl.BlockSpec(shape, lambda batch: (0,) * len(shape))
    return pl.pallas_call(
        middle_back_kernel,
        grid=(2,),
        out_shape=(
            shaped((2, rows, width), F32),
            shaped((2, rows, width), BF16),
            shaped((width, width), BF16),
            shaped((8, width), F32),
        ),
        in_specs=[row, row, row, pick(attn, 7), whole(gains)],
        out_specs=(row, row, still(width, width), still(8, width)),
        scratch_shapes=[pltpu.VMEM((width, width), F32)],
        compiler_params=params(),
        cost_estimate=cost(8 * rows * width * width, 12 << 20),
        name="middle_back",
    )(grad, r, o, attn, gains)


def device_index():
    return lax.axis_index("dp") * lax.axis_size("head") + lax.axis_index("head")


def swap(array, bit):
    count = lax.axis_size("dp") * lax.axis_size("head")
    return lax.ppermute(array, AXES, [(place, place ^ (1 << bit)) for place in range(count)])


def scatter_sum(stack, order):
    count = lax.axis_size("dp") * lax.axis_size("head")
    kinds, rows, columns = stack.shape
    here = device_index()
    current = stack.reshape(kinds, count, rows // count, columns)
    left = sorted(order)
    for bit in order:
        low = 1 << left.index(bit)
        left.remove(bit)
        high = current.shape[1] // (2 * low)
        view = current.reshape(kinds, high, 2, low, rows // count, columns)
        mine = (here >> bit) & 1
        kept = lax.dynamic_index_in_dim(view, mine, axis=2, keepdims=False)
        sent = lax.dynamic_index_in_dim(view, 1 - mine, axis=2, keepdims=False)
        total = kept.astype(F32) + swap(sent, bit).astype(F32)
        current = total.reshape(kinds, high * low, rows // count, columns)
        if left:
            current = current.astype(BF16)
    return current.reshape(kinds, rows // count, columns)


def sum_everywhere(array, bits):
    for bit in range(bits):
        array = array + swap(array, bit)
    return array


def body(
    source,
    target,
    cotangent,
    short_lengths,
    long_lengths,
    attn,
    ups,
    downs,
    gains,
    shifts,
):
    _, rows, width = source.shape
    devices = lax.axis_size("dp") * lax.axis_size("head")
    bits = devices.bit_length() - 1
    assert 2 * rows == LONG and rows % SHORT == 0 and devices == 1 << bits
    place = lax.axis_index("head")
    half = place % 2
    slots = rows // SHORT

    def biases(row, causal):
        short = lax.dynamic_slice_in_dim(short_lengths[row], place * slots, slots)
        bias_s = jnp.where(jnp.arange(SHORT)[None, :] < short[:, None], 0.0, MASKED).astype(F32)
        length = lax.dynamic_index_in_dim(long_lengths[row], place // 2, keepdims=False)
        position = jnp.arange(rows)
        own = position + half * rows < length
        other = position + (1 - half) * rows < length
        if causal:
            other = other & (half == 1)
        allowed = jnp.concatenate([own, other])[None, :]
        return bias_s, jnp.where(allowed, 0.0, MASKED).astype(F32)

    source_bias = biases(0, False)
    target_bias = biases(1, True)
    source_mate = swap(source[1], 0)
    target_mate = swap(target[1], 0)

    enc_saved = attend(source, None, source_mate, attn, 0, *source_bias, False)
    r1, u, r2, enc = feed(enc_saved[0], source, attn, ups, downs, gains, shifts)
    enc_mate = swap(enc[1], 0)
    self_saved = attend(target, None, target_mate, attn, 4, *target_bias, True)
    r3, h3 = middle(self_saved[0], target, attn, gains, shifts)
    cross_saved = attend(h3, enc, enc_mate, attn, 8, *source_bias, False)
    decoded, dr4, do_cross, dup1, ddown1, dw11, norms_a = turn(
        cross_saved[0], r3, cotangent, attn, ups, downs, gains, shifts
    )
    dh3, denc, denc_mate, dw8, dw9, dw10 = attend_back(
        do_cross, cross_saved, dr4, h3, enc, enc_mate, attn, 8
    )
    denc_mate = swap(denc_mate, 0)
    dr3, do_self, dw7, norms_b = middle_back(dh3, r3, self_saved[0], attn, gains)
    grad_target, dt_mate, dw4, dw5, dw6 = attend_back(
        do_self, self_saved, dr3, target, None, target_mate, attn, 4
    )
    dt_mate = swap(dt_mate, 0)
    dr1, do_enc, dup0, ddown0, dw3, norms_c = feed_back(
        denc, denc_mate, r2, r1, u, enc_saved[0], attn, ups, downs, gains, shifts
    )
    grad_source, ds_mate, dw0, dw1, dw2 = attend_back(
        do_enc, enc_saved, dr1, source, None, source_mate, attn, 0
    )
    ds_mate = swap(ds_mate, 0)
    grad_source = grad_source.at[1].add(ds_mate.astype(F32))
    grad_target = grad_target.at[1].add(dt_mate.astype(F32))

    first = tuple(range(bits))
    second = (0, 2, 1) + tuple(range(3, bits))
    up1 = scatter_sum(dup1[None], first)
    down1 = scatter_sum(ddown1[None], second)
    part_a = scatter_sum(jnp.stack([dw11, dw8]), first)
    part_b = scatter_sum(jnp.stack([dw9, dw10]), second)
    part_c = scatter_sum(jnp.stack([dw7, dw4]), first)
    part_d = scatter_sum(jnp.stack([dw5, dw6]), second)
    up0 = scatter_sum(dup0[None], first)
    down0 = scatter_sum(ddown0[None], second)
    part_e = scatter_sum(jnp.stack([dw3, dw0]), first)
    part_f = scatter_sum(jnp.stack([dw1, dw2]), second)
    grad_attn = jnp.stack(
        [
            part_e[1],
            part_f[0],
            part_f[1],
            part_e[0],
            part_c[1],
            part_d[0],
            part_d[1],
            part_c[0],
            part_a[1],
            part_b[0],
            part_b[1],
            part_a[0],
        ]
    )
    grad_up = jnp.concatenate([up0, up1])
    grad_down = jnp.concatenate([down0, down1])
    norms = jnp.stack(
        [
            norms_c[0],
            norms_c[2],
            norms_b[0],
            norms_a[2],
            norms_a[0],
            norms_c[1],
            norms_c[3],
            norms_b[1],
            norms_a[3],
            norms_a[1],
        ]
    )
    norms = sum_everywhere(norms, bits)
    share = width // devices
    norms = lax.dynamic_slice_in_dim(norms, device_index() * share, share, axis=1)
    return (
        decoded,
        grad_source,
        grad_target,
        grad_attn,
        grad_up,
        grad_down,
        norms[:5],
        norms[5:],
    )


def solution(mesh):
    rows = P(None, AXES, None)
    return jax.shard_map(
        body,
        mesh=mesh,
        in_specs=(rows, rows, rows, P(None, "dp"), P(None, "dp"), P(), P(), P(), P(), P()),
        out_specs=(rows, rows, rows, rows, rows, rows, P(None, AXES), P(None, AXES)),
        check_vma=False,
    )
```

time: 1850 us -> 443 us (0.24)
  matrix products: 471 us -> 0 us
  local copies, waits for them, and re-layouts: 460 us -> 16.2 us
  waiting for transfers between devices: 506 us -> 120 us
  starting transfers between devices: 279 us -> 71.3 us
  Pallas kernels: 0 us -> 195 us
  other arithmetic: 93.8 us -> 31.4 us
    dot_general x220 -> x0, matrix products: 414 us -> none  [the longest x60 141 us: matmul(): return jnp.dot(operand, weight, preferred_element_type=jnp.float32)]
    reduce_scatter x3 -> x0, waiting for transfers between devices: 311 us -> none  [the longest x1 158 us: body(): lax.psum_scatter(summed[0], ('dp', 'head'), scatter_dimension=1, tiled=True)]
    all_to_all x72 -> x0, starting transfers between devices: 278 us -> none  [the longest x12 48.2 us: attention_forward(): lax.all_to_all(output_head, 'head', split_axis=0, concat_axis=1, tiled=True)]
    pallas_call x0 -> x11, Pallas kernels: none -> 195 us  [the longest x3 74.4 us: attend_back(): pl.pallas_call(functools.partial(attend_back_kernel, self_keys), grid=(wi...]
    all_to_all x72 -> x0, waiting for transfers between devices: 194 us -> none  [the longest x12 53.8 us: attention_forward(): lax.all_to_all(split_heads(value_flat), 'head', split_axis=1, concat_axis...]
    unnamed x749 -> x87, local copies, waits for them, and re-layouts: 130 us -> 1.53 us
    ppermute x0 -> x61, waiting for transfers between devices: none -> 120 us  [swap(): lax.ppermute(array, AXES, [(place, place ^ 1 << bit) for place in range(c...]
    all_to_all x102 -> x0, local copies, waits for them, and re-layouts: 115 us -> none  [the longest x24 27.4 us: attention_forward(): lax.all_to_all(output_head, 'head', split_axis=0, concat_axis=1, tiled=True)]
  transfers between devices with their start and end apart: 77 -> 61, of which waited for: 39 -> 34; matrix products, arithmetic and copies ran while one was open for 52% -> 10% of each run, Pallas kernels for 0% -> 28%
where the time goes in v1:
time: 443 us; the launch traced here: 436 us
  Pallas kernels  195 us (44%)
  waiting for transfers between devices  120 us (27%)
  starting transfers between devices  71.3 us (16%)
  other arithmetic  31.4 us (7%)
  local copies, waits for them, and re-layouts  16.2 us (4%)
    ppermute x61, waiting for transfers between devices, swap(): lax.ppermute(array, AXES, [(place, place ^ 1 << bit) for place in range(c...  120 us
    pallas_call x3, Pallas kernels, attend_back(): pl.pallas_call(functools.partial(attend_back_kernel, self_keys), grid=(wi...  74.4 us
    ppermute x61, starting transfers between devices, swap(): lax.ppermute(array, AXES, [(place, place ^ 1 << bit) for place in range(c...  71.3 us
    pallas_call x3, Pallas kernels, attend(): pl.pallas_call(functools.partial(attend_kernel, causal, self_keys), grid=...  46.7 us
    pallas_call x1, Pallas kernels, turn(): pl.pallas_call(functools.partial(turn_kernel, inner // CHUNK), grid=(2,),...  27.1 us
    pallas_call x1, Pallas kernels, feed_back(): pl.pallas_call(functools.partial(feed_back_kernel, inner // CHUNK), grid=...  24.5 us
    convert_element_type x40, other arithmetic, scatter_sum(): current = current.astype(BF16)  15.4 us
    pallas_call x1, Pallas kernels, feed(): pl.pallas_call(functools.partial(feed_kernel, inner // CHUNK), grid=(2,),...  12.2 us
  transfers between devices with their start and end apart: 61, of which 34 were waited for; matrix products, arithmetic and copies ran while one was open for 10% of the time, Pallas kernels for 28%

profile of v1, /device:TPU:0, one launch (start us, length us, event | category | flops | bytes accessed | tf_op | source)
XLA Modules:
  0.0 435.7 jit_solution(12615079217789827276)
XLA Ops:
  10.0 15.4 %attend.4 = (bf16[2,512,512]{2,1,0:T(8,128)(2,1)}, f32[2,512,512]{2,1,0:T(8,128)}, bf16[2,512,512]{2,1,0:T(8,128)(2,1)}, bf16[512,512]{1,0:T(8,128)(2,1)}, bf16[...) custom-call(bf16[2,512,512]{2,1,0:T(8,128)(2,1)} %refs_11_.2, ...), custom_call_target="tpu_custom_call" | custom-call | flops 6442450944 | bytes 23068672 | tf_op jit(solution)/shard_map/attend/pallas_call | solution.py:150
  25.4 12.2 %feed.1 = (f32[2,512,512]{2,1,0:T(8,128)}, f32[2,512,2048]{2,1,0:T(8,128)}, f32[2,512,512]{2,1,0:T(8,128)}, bf16[2,512,512]{2,1,0:T(8,128)(2,1)}) custom-call(bf16[2,512,512]{2,1,0:T(8,128)(2,1)} %get-tuple-element.100.o_ref.refs_1_, bf16[2,512,512]{2,1,0:T(8,128)(2,1)} %refs_11_.2, bf16[12,512,512]{2,1,0:T(8,128)(2,1)} %refs_15_.5, ...), custom_call_target="tpu_custom_call" | custom-call | flops 4831838208 | bytes 23068672 | tf_op jit(solution)/shard_map/feed/pallas_call | solution.py:381
  37.5 1.9 slice_bitcast_fusion
  39.8 15.9 %attend.3 = (bf16[2,512,512]{2,1,0:T(8,128)(2,1)}, f32[2,512,512]{2,1,0:T(8,128)}, bf16[2,512,512]{2,1,0:T(8,128)(2,1)}, bf16[512,512]{1,0:T(8,128)(2,1)}, bf16[...) custom-call(bf16[2,512,512]{2,1,0:T(8,128)(2,1)} %refs_11_.3, ...), custom_call_target="tpu_custom_call" | custom-call | flops 6442450944 | bytes 23068672 | tf_op jit(solution)/shard_map/attend/pallas_call | solution.py:150
  55.7 3.7 middle.1
  59.4 15.5 %attend.5 = (bf16[2,512,512]{2,1,0:T(8,128)(2,1)}, f32[2,512,512]{2,1,0:T(8,128)}, bf16[2,512,512]{2,1,0:T(8,128)(2,1)}, bf16[512,512]{1,0:T(8,128)(2,1)}, bf16[...) custom-call(bf16[2,512,512]{2,1,0:T(8,128)(2,1)} %get-tuple-element., ...), custom_call_target="tpu_custom_call" | custom-call | flops 6442450944 | bytes 23068672 | tf_op jit(solution)/shard_map/attend/pallas_call | solution.py:150
  74.9 27.1 %turn.1 = (bf16[2,512,512]{2,1,0:T(8,128)(2,1)}, f32[2,512,512]{2,1,0:T(8,128)}, bf16[2,512,512]{2,1,0:T(8,128)(2,1)}, bf16[512,2048]{1,0:T(8,128)(2,1)}, bf16[2...) custom-call(bf16[2,512,512]{2,1,0:T(8,128)(2,1)} %get-tuple-element.102.o_ref.refs_1_, ...), custom_call_target="tpu_custom_call" | custom-call | flops 14495514624 | bytes 20971520 | tf_op jit(solution)/shard_map/turn/pallas_call | solution.py:516
  102.0 25.7 %attend_back.3 = (f32[2,512,512]{2,1,0:T(8,128)}, f32[2,512,512]{2,1,0:T(8,128)}, bf16[512,512]{1,0:T(8,128)(2,1)}, bf16[512,512]{1,0:T(8,128)(2,1)}, bf16[512,5...) custom-call(bf16[2,512,512]{2,1,0:T(8,128)(2,1)} %get-tuple-element.105.refs_0_, ...), custom_call_target="tpu_custom_call" | custom-call | flops 12884901888 | bytes 29360128 | tf_op jit(solution)/shard_map/attend_back/pallas_call | solution.py:312
  127.7 6.4 %middle_back.1 = (f32[2,512,512]{2,1,0:T(8,128)}, bf16[2,512,512]{2,1,0:T(8,128)(2,1)}, bf16[512,512]{1,0:T(8,128)(2,1)}, f32[8,512]{1,0:T(8,128)}) custom-call(f32[2,512,512]{2,1,0:T(8,128)} %get-tuple-element.132.grad_ref, f32[2,512,512]{2,1,0:T(8,128)} %get-tuple-element.103.r3_ref.r_ref, bf16[2,512,512]{2,1,0:T(8,128)(2,1)} %get-tuple-element.98.o_ref.refs_1_, ...), custom_call_target="tpu_custom_call" | custom-call | flops 1073741824 | bytes 12582912 | tf_op jit(solution)/shard_map/middle_back/pallas_call | solution.py:662
  134.3 2.4 dynamic-slice_bitcast_fusion
  140.5 24.4 %attend_back.5 = (f32[2,512,512]{2,1,0:T(8,128)}, bf16[512,512]{1,0:T(8,128)(2,1)}, bf16[512,512]{1,0:T(8,128)(2,1)}, bf16[512,512]{1,0:T(8,128)(2,1)}, bf16[512,512]{1,0:T(8,128)(2,1)}) custom-call(bf16[2,512,512]{2,1,0:T(8,128)(2,1)} %get-tuple-element.133.refs_0_, bf16[2,512,512]{2,1,0:T(8,128)(2,1)} %get-tuple-element.98.o_ref.refs_1_, ...), custom_call_target="tpu_custom_call" | custom-call | flops 12884901888 | bytes 29360128 | tf_op jit(solution)/shard_map/attend_back/pallas_call | solution.py:312
  164.9 1.9 fusion.25
  166.8 1.8 fusion.29
  169.9 24.5 %feed_back.1 = (f32[2,512,512]{2,1,0:T(8,128)}, bf16[2,512,512]{2,1,0:T(8,128)(2,1)}, bf16[512,2048]{1,0:T(8,128)(2,1)}, bf16[2048,512]{1,0:T(8,128)(2,1)}, bf16[512,512]{1,0:T(8,128)(2,1)}, /*index=5*/f32[8,512]{1,0:T(8,128)}) custom-call(f32[2,512,512]{2,1,0:T(8,128)} %get-tuple-element.115.grad_ref, bf16[512,512]{1,0:T(8,128)(2,1)} %collective-permute-done.3.mate_ref, ...), custom_call_target="tpu_custom_call" | custom-call | flops 9663676416 | bytes 31457280 | tf_op jit(solution)/shard_map/feed_back/pallas_call | solution.py:607
  194.4 2.5 dynamic-slice_bitcast_fusion.3
  199.0 2.1 fusion.9
  202.7 2.2 fusion.10
  206.1 2.9 collective-permute-start.32
  211.6 24.4 %attend_back.4 = (f32[2,512,512]{2,1,0:T(8,128)}, bf16[512,512]{1,0:T(8,128)(2,1)}, bf16[512,512]{1,0:T(8,128)(2,1)}, bf16[512,512]{1,0:T(8,128)(2,1)}, bf16[512,512]{1,0:T(8,128)(2,1)}) custom-call(bf16[2,512,512]{2,1,0:T(8,128)(2,1)} %get-tuple-element.120.refs_0_, bf16[2,512,512]{2,1,0:T(8,128)(2,1)} %get-tuple-element.100.o_ref.refs_1_, ...), custom_call_target="tpu_custom_call" | custom-call | flops 12884901888 | bytes 29360128 | tf_op jit(solution)/shard_map/attend_back/pallas_call | solution.py:312
  241.3 3.9 collective-permute-done.58
  246.8 2.3 collective-permute-done.59
  249.1 2.6 collective-permute-start.60
  251.7 2.2 collective-permute-done.60
  257.7 5.0 %collective-permute-done.27 = bf16[2,8,1,16,512]{4,3,1,0,2:T(8,128)(2,1)S(1)} collective-permute-done((bf16[2,8,1,16,512]{4,3,1,0,2:T(8,128)(2,1)S(1)}, bf16[2,8,1,16,512]{4,3,1,0,2:T(8,128)(2,1)S(1)}, u32[]{:S(2)}, u32[]{:S(2)}) %collective-permute-start.27) | collective-permute-done | bytes 262176 | tf_op jit(solution)/shard_map/ppermute | solution.py:686
  264.6 5.8 %collective-permute-done.17 = bf16[2,8,1,16,512]{4,3,1,0,2:T(8,128)(2,1)S(1)} collective-permute-done((bf16[2,8,1,16,512]{4,3,1,0,2:T(8,128)(2,1)S(1)}, bf16[2,8,1,16,512]{4,3,1,0,2:T(8,128)(2,1)S(1)}, u32[]{:S(2)}, u32[]{:S(2)}) %collective-permute-start.17) | collective-permute-done | bytes 262176 | tf_op jit(solution)/shard_map/ppermute | solution.py:686
  272.1 3.2 collective-permute-done.33
  275.6 4.7 %collective-permute-done.28 = bf16[2,4,1,16,512]{4,3,1,0,2:T(8,128)(2,1)S(1)} collective-permute-done((bf16[2,4,1,16,512]{4,3,1,0,2:T(8,128)(2,1)S(1)}, bf16[2,4,1,16,512]{4,3,1,0,2:T(8,128)(2,1)S(1)}, u32[]{:S(2)}, u32[]{:S(2)}) %collective-permute-start.28) | collective-permute-done | bytes 131104 | tf_op jit(solution)/shard_map/ppermute | solution.py:686
  280.3 2.2 collective-permute-start.23
  282.6 2.9 collective-permute-done.23
  286.2 4.3 collective-permute-done.18
  292.0 3.1 collective-permute-done.34
  296.6 3.1 collective-permute-done.29
  301.2 2.7 collective-permute-done.24
  305.5 2.7 collective-permute-done.19
  308.2 2.3 collective-permute-start.35
  310.6 2.5 collective-permute-done.35
  313.1 2.3 collective-permute-start.30
  315.3 2.5 collective-permute-done.30
  317.9 2.3 collective-permute-start.25
  320.1 2.5 collective-permute-done.25
  322.7 2.3 collective-permute-start.20
  325.0 2.5 collective-permute-done.20
  328.1 1.7 fusion
  330.0 1.7 fusion.2
  335.7 16.9 %collective-permute-done.7 = bf16[2,8,1,16,512]{4,3,1,0,2:T(8,128)(2,1)S(1)} collective-permute-done((bf16[2,8,1,16,512]{4,3,1,0,2:T(8,128)(2,1)S(1)}, bf16[2,8,1,16,512]{4,3,1,0,2:T(8,128)(2,1)S(1)}, u32[]{:S(2)}, u32[]{:S(2)}) %collective-permute-start.7) | collective-permute-done | bytes 262176 | tf_op jit(solution)/shard_map/ppermute | solution.py:686
  353.9 6.1 %collective-permute-done.12 = bf16[2,4,2,16,512]{4,3,2,1,0:T(8,128)(2,1)S(1)} collective-permute-done((bf16[2,4,2,16,512]{4,3,2,1,0:T(8,128)(2,1)S(1)}, bf16[2,4,2,16,512]{4,3,2,1,0:T(8,128)(2,1)S(1)}, u32[]{:S(2)}, u32[]{:S(2)}) %collective-permute-start.12) | collective-permute-done | bytes 262176 | tf_op jit(solution)/shard_map/ppermute | solution.py:686
  361.4 3.6 collective-permute-done.8
  366.2 3.8 collective-permute-done.13
  371.2 3.0 collective-permute-done.9
  375.4 3.1 collective-permute-done.14
  378.5 2.0 collective-permute-start.10
  380.5 2.8 collective-permute-done.10
  383.3 2.0 collective-permute-start.15
  385.3 2.8 collective-permute-done.15
  388.3 1.7 fusion.1
  395.2 6.9 %collective-permute-done.43 = bf16[1,4,1,16,2048]{4,3,1,2,0:T(8,128)(2,1)S(1)} collective-permute-done((bf16[1,4,1,16,2048]{4,3,1,2,0:T(8,128)(2,1)S(1)}, bf16[1,4,1,16,2048]{4,3,1,2,0:T(8,128)(2,1)S(1)}, u32[]{:S(2)}, u32[]{:S(2)}) %collective-permute-start.43) | collective-permute-done | bytes 262176 | tf_op jit(solution)/shard_map/ppermute | solution.py:686
  404.5 2.8 collective-permute-done.44
  407.3 2.1 collective-permute-start.45
  409.5 2.1 collective-permute-start.55
  411.6 1.7 collective-permute-done.45
  415.0 1.7 collective-permute-start.48
  418.5 3.0 collective-permute-done.48
  421.6 2.6 collective-permute-start.49
  427.2 2.3 collective-permute-start.50
  (290 shorter events, 74.7 us)
Async XLA Ops:
  1.7 8.3 %collective-permute-start.1 = (bf16[512,512]{1,0:T(8,128)(2,1)S(1)}, bf16[512,512]{1,0:T(8,128)(2,1)}, u32[]{:S(2)}, u32[]{:S(2)}) collective-permute-start(bf16[512,512]{1,0:T(8,128)(2,1)S(1)} %slice_bitcast_fusion.1), channel_id=1, source_target_pairs={{0,1},{1,0},{2,3},{3,2},{4,5},{5,4},{6,7},{7,6},{8,9},{9,8},{10,11... | collective-permute-start | bytes 1572872 | tf_op jit(solution)/shard_map/ppermute | solution.py:686
  3.3 36.5 %collective-permute-start = (bf16[512,512]{1,0:T(8,128)(2,1)S(1)}, bf16[512,512]{1,0:T(8,128)(2,1)}, u32[]{:S(2)}, u32[]{:S(2)}) collective-permute-start(bf16[512,512]{1,0:T(8,128)(2,1)S(1)} %slice_bitcast_fusion.2), channel_id=1, source_target_pairs={{0,1},{1,0},{2,3},{3,2},{4,5},{5,4},{6,7},{7,6},{8,9},{9,8},{10,11... | collective-permute-start | bytes 1572872 | tf_op jit(solution)/shard_map/ppermute | solution.py:686
  39.4 20.0 %collective-permute-start.2 = (bf16[512,512]{1,0:T(8,128)(2,1)}, bf16[512,512]{1,0:T(8,128)(2,1)}, u32[]{:S(2)}, u32[]{:S(2)}) collective-permute-start(bf16[512,512]{1,0:T(8,128)(2,1)} %slice_bitcast_fusion), channel_id=1, source_target_pairs={{0,1},{1,0},{2,3},{3,2},{4,5},{5,4},{6,7},{7,6},{8,9},{9,8},{10,11... | collective-permute-start | bytes 1572872 | tf_op jit(solution)/shard_map/ppermute | solution.py:686
  134.1 35.3 %collective-permute-start.3 = (bf16[512,512]{1,0:T(8,128)(2,1)}, bf16[512,512]{1,0:T(8,128)(2,1)}, u32[]{:S(2)}, u32[]{:S(2)}) collective-permute-start(bf16[512,512]{1,0:T(8,128)(2,1)} %get-tuple-element.116), channel_id=1, source_target_pairs={{0,1},{1,0},{2,3},{3,2},{4,5},{5,4},{6,7},{7,6},{8,9},{9,8},{10,11... | collective-permute-start | bytes 1572872 | tf_op jit(solution)/shard_map/ppermute | solution.py:686
  136.7 190.8 %collective-permute-start.51 = (bf16[1,16,1,64,512]{4,3,1,2,0:T(8,128)(2,1)}, bf16[1,16,1,64,512]{4,3,1,2,0:T(8,128)(2,1)}, u32[]{:S(2)}, u32[]{:S(2)}) collective-permute-start(bf16[1,16,1,64,512]{4,3,1,2,0:T(8,128)(2,1)} %dynamic-slice_bitcast_fusion), channel_id=1, source_target_pairs={{0,1},{1,0},{2,3},{3,2},{4,5},{5,4},{6,7},{7,6},{8,9},{9,8},{10,11... | collective-permute-start | bytes 3145736 | tf_op jit(solution)/shard_map/ppermute | solution.py:686
  138.2 191.8 %collective-permute-start.41 = (bf16[1,16,1,16,2048]{4,3,1,2,0:T(8,128)(2,1)}, bf16[1,16,1,16,2048]{4,3,1,2,0:T(8,128)(2,1)}, u32[]{:S(2)}, u32[]{:S(2)}) collective-permute-start(bf16[1,16,1,16,2048]{4,3,1,2,0:T(8,128)(2,1)} %dynamic-slice_bitcast_fusion.2), channel_id=1, source_target_pairs={{0,1},{1,0},{2,3},{3,2},{4,5},{5,4},{6,7},{7,6},{8,9},{9,8},{10,11... | collective-permute-start | bytes 3145736 | tf_op jit(solution)/shard_map/ppermute | solution.py:686
  139.1 57.8 %collective-permute-start.31 = (bf16[2,16,1,16,512]{4,3,1,0,2:T(8,128)(2,1)}, bf16[2,16,1,16,512]{4,3,1,0,2:T(8,128)(2,1)}, u32[]{:S(2)}, u32[]{:S(2)}) collective-permute-start(bf16[2,16,1,16,512]{4,3,1,0,2:T(8,128)(2,1)} %fusion.17), channel_id=1, source_target_pairs={{0,1},{1,0},{2,3},{3,2},{4,5},{5,4},{6,7},{7,6},{8,9},{9,8},{10,11... | collective-permute-start | bytes 1572872 | tf_op jit(solution)/shard_map/ppermute | solution.py:686
  140.4 58.0 %collective-permute-start.26 = (bf16[2,16,1,16,512]{4,3,1,0,2:T(8,128)(2,1)}, bf16[2,16,1,16,512]{4,3,1,0,2:T(8,128)(2,1)}, u32[]{:S(2)}, u32[]{:S(2)}) collective-permute-start(bf16[2,16,1,16,512]{4,3,1,0,2:T(8,128)(2,1)} %fusion.21), channel_id=1, source_target_pairs={{0,1},{1,0},{2,3},{3,2},{4,5},{5,4},{6,7},{7,6},{8,9},{9,8},{10,11... | collective-permute-start | bytes 1572872 | tf_op jit(solution)/shard_map/ppermute | solution.py:686
  169.4 32.9 %collective-permute-start.21 = (bf16[2,16,1,16,512]{4,3,1,0,2:T(8,128)(2,1)}, bf16[2,16,1,16,512]{4,3,1,0,2:T(8,128)(2,1)}, u32[]{:S(2)}, u32[]{:S(2)}) collective-permute-start(bf16[2,16,1,16,512]{4,3,1,0,2:T(8,128)(2,1)} %fusion.25), channel_id=1, source_target_pairs={{0,1},{1,0},{2,3},{3,2},{4,5},{5,4},{6,7},{7,6},{8,9},{9,8},{10,11... | collective-permute-start | bytes 1572872 | tf_op jit(solution)/shard_map/ppermute | solution.py:686
  196.9 8.0 %collective-permute-start.16 = (bf16[2,16,1,16,512]{4,3,1,0,2:T(8,128)(2,1)}, bf16[2,16,1,16,512]{4,3,1,0,2:T(8,128)(2,1)S(1)}, u32[]{:S(2)}, u32[]{:S(2)}) collective-permute-start(bf16[2,16,1,16,512]{4,3,1,0,2:T(8,128)(2,1)} %fusion.29), channel_id=1, source_target_pairs={{0,1},{1,0},{2,3},{3,2},{4,5},{5,4},{6,7},{7,6},{8,9},{9,8},{10,11... | collective-permute-start | bytes 1572872 | tf_op jit(solution)/shard_map/ppermute | solution.py:686
  198.5 7.6 %collective-permute-start.5 = (bf16[512,512]{1,0:T(8,128)(2,1)}, bf16[512,512]{1,0:T(8,128)(2,1)}, u32[]{:S(2)}, u32[]{:S(2)}) collective-permute-start(bf16[512,512]{1,0:T(8,128)(2,1)} %get-tuple-element.144), channel_id=1, source_target_pairs={{0,1},{1,0},{2,3},{3,2},{4,5},{5,4},{6,7},{7,6},{8,9},{9,8},{10,11... | collective-permute-start | bytes 1572872 | tf_op jit(solution)/shard_map/ppermute | solution.py:686
  202.3 35.0 %collective-permute-start.56 = (f32[10,512]{1,0:T(8,128)S(1)}, f32[10,512]{1,0:T(8,128)S(1)}, u32[]{:S(2)}, u32[]{:S(2)}) collective-permute-start(f32[10,512]{1,0:T(8,128)S(1)} %stack.79), channel_id=1, source_target_pairs={{0,1},{1,0},{2,3},{3,2},{4,5},{5,4},{6,7},{7,6},{8,9},{9,8},{10,11... | collective-permute-start | bytes 61448 | tf_op jit(solution)/shard_map/ppermute | solution.py:686
  204.9 183.4 %collective-permute-start.46 = (bf16[1,16,1,64,512]{4,3,1,2,0:T(8,128)(2,1)}, bf16[1,16,1,64,512]{4,3,1,2,0:T(8,128)(2,1)}, u32[]{:S(2)}, u32[]{:S(2)}) collective-permute-start(bf16[1,16,1,64,512]{4,3,1,2,0:T(8,128)(2,1)} %dynamic-slice_bitcast_fusion.1), channel_id=1, source_target_pairs={{0,1},{1,0},{2,3},{3,2},{4,5},{5,4},{6,7},{7,6},{8,9},{9,8},{10,11... | collective-permute-start | bytes 3145736 | tf_op jit(solution)/shard_map/ppermute | solution.py:686
  206.1 50.0 %collective-permute-start.32 = (bf16[2,4,2,16,512]{4,3,2,1,0:T(8,128)(2,1)S(1)}, bf16[2,4,2,16,512]{4,3,2,1,0:T(8,128)(2,1)}, u32[]{:S(2)}, u32[]{:S(2)}) collective-permute-start(bf16[2,4,2,16,512]{4,3,2,1,0:T(8,128)(2,1)S(1)} %dynamic-slice_bitcast_fusion.10), channel_id=1, source_target_pairs={{0,4},{1,5},{2,6},{3,7},{4,0},{5,1},{6,2},{7,3},{8,12},{9,13},{10,... | collective-permute-start | bytes 786440 | tf_op jit(solution)/shard_map/ppermute | solution.py:686
  237.3 4.0 collective-permute-start.57
  241.3 3.9 collective-permute-start.58
  245.2 3.9 collective-permute-start.59
  249.1 4.8 %collective-permute-start.60 = (f32[10,512]{1,0:T(8,128)S(1)}, f32[10,512]{1,0:T(8,128)S(1)}, u32[]{:S(2)}, u32[]{:S(2)}) collective-permute-start(f32[10,512]{1,0:T(8,128)S(1)} %add.463), channel_id=1, source_target_pairs={{0,16},{1,17},{2,18},{3,19},{4,20},{5,21},{6,22},{7,23},{8,24},{9,... | collective-permute-start | bytes 61448 | tf_op jit(solution)/shard_map/ppermute | solution.py:686
  253.9 8.8 %collective-permute-start.27 = (bf16[2,8,1,16,512]{4,3,1,0,2:T(8,128)(2,1)S(1)}, bf16[2,8,1,16,512]{4,3,1,0,2:T(8,128)(2,1)S(1)}, u32[]{:S(2)}, u32[]{:S(2)}) collective-permute-start(bf16[2,8,1,16,512]{4,3,1,0,2:T(8,128)(2,1)S(1)} %dynamic-slice_bitcast_fusion.11), channel_id=1, source_target_pairs={{0,2},{1,3},{2,0},{3,1},{4,6},{5,7},{6,4},{7,5},{8,10},{9,11},{10,... | collective-permute-start | bytes 786440 | tf_op jit(solution)/shard_map/ppermute | solution.py:686
  256.1 8.2 %collective-permute-start.22 = (bf16[2,4,2,16,512]{4,3,2,1,0:T(8,128)(2,1)S(1)}, bf16[2,4,2,16,512]{4,3,2,1,0:T(8,128)(2,1)S(1)}, u32[]{:S(2)}, u32[]{:S(2)}) collective-permute-start(bf16[2,4,2,16,512]{4,3,2,1,0:T(8,128)(2,1)S(1)} %dynamic-slice_bitcast_fusion.12), channel_id=1, source_target_pairs={{0,4},{1,5},{2,6},{3,7},{4,0},{5,1},{6,2},{7,3},{8,12},{9,13},{10,... | collective-permute-start | bytes 786440 | tf_op jit(solution)/shard_map/ppermute | solution.py:686
  262.7 7.7 %collective-permute-start.17 = (bf16[2,8,1,16,512]{4,3,1,0,2:T(8,128)(2,1)S(1)}, bf16[2,8,1,16,512]{4,3,1,0,2:T(8,128)(2,1)S(1)}, u32[]{:S(2)}, u32[]{:S(2)}) collective-permute-start(bf16[2,8,1,16,512]{4,3,1,0,2:T(8,128)(2,1)S(1)} %dynamic-slice_bitcast_fusion.13), channel_id=1, source_target_pairs={{0,2},{1,3},{2,0},{3,1},{4,6},{5,7},{6,4},{7,5},{8,10},{9,11},{10,... | collective-permute-start | bytes 786440 | tf_op jit(solution)/shard_map/ppermute | solution.py:686
  264.4 129.4 %collective-permute-start.36 = (bf16[1,16,1,16,2048]{4,3,1,2,0:T(8,128)(2,1)S(1)}, bf16[1,16,1,16,2048]{4,3,1,2,0:T(8,128)(2,1)S(1)}, u32[]{:S(2)}, u32[]{:S(2)}) collective-permute-start(bf16[1,16,1,16,2048]{4,3,1,2,0:T(8,128)(2,1)S(1)} %copy-done.27), channel_id=1, source_target_pairs={{0,1},{1,0},{2,3},{3,2},{4,5},{5,4},{6,7},{7,6},{8,9},{9,8},{10,11... | collective-permute-start | bytes 3145736 | tf_op jit(solution)/shard_map/ppermute | solution.py:686
  270.4 5.0 %collective-permute-start.33 = (bf16[2,4,1,16,512]{4,3,2,1,0:T(8,128)(2,1)S(1)}, bf16[2,4,1,16,512]{4,3,2,1,0:T(8,128)(2,1)S(1)}, u32[]{:S(2)}, u32[]{:S(2)}) collective-permute-start(bf16[2,4,1,16,512]{4,3,2,1,0:T(8,128)(2,1)S(1)} %constant_dynamic-slice_fusion.8), channel_id=1, source_target_pairs={{0,2},{1,3},{2,0},{3,1},{4,6},{5,7},{6,4},{7,5},{8,10},{9,11},{10,... | collective-permute-start | bytes 393224 | tf_op jit(solution)/shard_map/ppermute | solution.py:686
  272.1 56.0 %copy-start.26 = (bf16[2048,512]{1,0:T(8,128)(2,1)S(1)}, bf16[2048,512]{1,0:T(8,128)(2,1)}, u32[]{:S(2)}) copy-start(bf16[2048,512]{1,0:T(8,128)(2,1)} %get-tuple-element.160) | copy-start | bytes 6291460
  275.3 5.0 %collective-permute-start.28 = (bf16[2,4,1,16,512]{4,3,1,0,2:T(8,128)(2,1)S(1)}, bf16[2,4,1,16,512]{4,3,1,0,2:T(8,128)(2,1)S(1)}, u32[]{:S(2)}, u32[]{:S(2)}) collective-permute-start(bf16[2,4,1,16,512]{4,3,1,0,2:T(8,128)(2,1)S(1)} %dynamic-slice_bitcast_fusion.20), channel_id=1, source_target_pairs={{0,4},{1,5},{2,6},{3,7},{4,0},{5,1},{6,2},{7,3},{8,12},{9,13},{10,... | collective-permute-start | bytes 393224 | tf_op jit(solution)/shard_map/ppermute | solution.py:686
  280.3 5.2 %collective-permute-start.23 = (bf16[2,4,1,16,512]{4,3,2,1,0:T(8,128)(2,1)S(1)}, bf16[2,4,1,16,512]{4,3,2,1,0:T(8,128)(2,1)S(1)}, u32[]{:S(2)}, u32[]{:S(2)}) collective-permute-start(bf16[2,4,1,16,512]{4,3,2,1,0:T(8,128)(2,1)S(1)} %constant_dynamic-slice_fusion.12), channel_id=1, source_target_pairs={{0,2},{1,3},{2,0},{3,1},{4,6},{5,7},{6,4},{7,5},{8,10},{9,11},{10,... | collective-permute-start | bytes 393224 | tf_op jit(solution)/shard_map/ppermute | solution.py:686
  285.5 5.0 %collective-permute-start.18 = (bf16[2,4,1,16,512]{4,3,1,0,2:T(8,128)(2,1)S(1)}, bf16[2,4,1,16,512]{4,3,1,0,2:T(8,128)(2,1)S(1)}, u32[]{:S(2)}, u32[]{:S(2)}) collective-permute-start(bf16[2,4,1,16,512]{4,3,1,0,2:T(8,128)(2,1)S(1)} %dynamic-slice_bitcast_fusion.21), channel_id=1, source_target_pairs={{0,4},{1,5},{2,6},{3,7},{4,0},{5,1},{6,2},{7,3},{8,12},{9,13},{10,... | collective-permute-start | bytes 393224 | tf_op jit(solution)/shard_map/ppermute | solution.py:686
  290.5 4.6 %collective-permute-start.34 = (bf16[2,2,1,16,512]{4,3,2,1,0:T(8,128)(2,1)S(1)}, bf16[2,2,1,16,512]{4,3,2,1,0:T(8,128)(2,1)S(1)}, u32[]{:S(2)}, u32[]{:S(2)}) collective-permute-start(bf16[2,2,1,16,512]{4,3,2,1,0:T(8,128)(2,1)S(1)} %dynamic-slice_bitcast_fusion.23), channel_id=1, source_target_pairs={{0,8},{1,9},{2,10},{3,11},{4,12},{5,13},{6,14},{7,15},{8,0},{9,1},... | collective-permute-start | bytes 196616 | tf_op jit(solution)/shard_map/ppermute | solution.py:686
  295.1 4.6 %collective-permute-start.29 = (bf16[2,2,1,16,512]{4,3,2,1,0:T(8,128)(2,1)S(1)}, bf16[2,2,1,16,512]{4,3,2,1,0:T(8,128)(2,1)S(1)}, u32[]{:S(2)}, u32[]{:S(2)}) collective-permute-start(bf16[2,2,1,16,512]{4,3,2,1,0:T(8,128)(2,1)S(1)} %dynamic-slice_bitcast_fusion.24), channel_id=1, source_target_pairs={{0,8},{1,9},{2,10},{3,11},{4,12},{5,13},{6,14},{7,15},{8,0},{9,1},... | collective-permute-start | bytes 196616 | tf_op jit(solution)/shard_map/ppermute | solution.py:686
  299.7 4.3 collective-permute-start.24
  304.0 4.3 collective-permute-start.19
  308.2 4.8 %collective-permute-start.35 = (bf16[2,1,1,16,512]{4,3,2,1,0:T(8,128)(2,1)S(1)}, bf16[2,1,1,16,512]{4,3,2,1,0:T(8,128)(2,1)S(1)}, u32[]{:S(2)}, u32[]{:S(2)}) collective-permute-start(bf16[2,1,1,16,512]{4,3,2,1,0:T(8,128)(2,1)S(1)} %constant_dynamic-slice_fusion.7), channel_id=1, source_target_pairs={{0,16},{1,17},{2,18},{3,19},{4,20},{5,21},{6,22},{7,23},{8,24},{9,... | collective-permute-start | bytes 98312 | tf_op jit(solution)/shard_map/ppermute | solution.py:686
  313.1 4.8 %collective-permute-start.30 = (bf16[2,1,1,16,512]{4,3,2,1,0:T(8,128)(2,1)S(1)}, bf16[2,1,1,16,512]{4,3,2,1,0:T(8,128)(2,1)S(1)}, u32[]{:S(2)}, u32[]{:S(2)}) collective-permute-start(bf16[2,1,1,16,512]{4,3,2,1,0:T(8,128)(2,1)S(1)} %constant_dynamic-slice_fusion.10), channel_id=1, source_target_pairs={{0,16},{1,17},{2,18},{3,19},{4,20},{5,21},{6,22},{7,23},{8,24},{9,... | collective-permute-start | bytes 98312 | tf_op jit(solution)/shard_map/ppermute | solution.py:686
  317.9 4.8 %collective-permute-start.25 = (bf16[2,1,1,16,512]{4,3,2,1,0:T(8,128)(2,1)S(1)}, bf16[2,1,1,16,512]{4,3,2,1,0:T(8,128)(2,1)S(1)}, u32[]{:S(2)}, u32[]{:S(2)}) collective-permute-start(bf16[2,1,1,16,512]{4,3,2,1,0:T(8,128)(2,1)S(1)} %constant_dynamic-slice_fusion.11), channel_id=1, source_target_pairs={{0,16},{1,17},{2,18},{3,19},{4,20},{5,21},{6,22},{7,23},{8,24},{9,... | collective-permute-start | bytes 98312 | tf_op jit(solution)/shard_map/ppermute | solution.py:686
  322.7 4.8 %collective-permute-start.20 = (bf16[2,1,1,16,512]{4,3,2,1,0:T(8,128)(2,1)S(1)}, bf16[2,1,1,16,512]{4,3,2,1,0:T(8,128)(2,1)S(1)}, u32[]{:S(2)}, u32[]{:S(2)}) collective-permute-start(bf16[2,1,1,16,512]{4,3,2,1,0:T(8,128)(2,1)S(1)} %constant_dynamic-slice_fusion.13), channel_id=1, source_target_pairs={{0,16},{1,17},{2,18},{3,19},{4,20},{5,21},{6,22},{7,23},{8,24},{9,... | collective-permute-start | bytes 98312 | tf_op jit(solution)/shard_map/ppermute | solution.py:686
  327.5 4.3 collective-permute-start.11
  327.5 5.4 %collective-permute-start.6 = (bf16[2,16,1,16,512]{4,3,1,0,2:T(8,128)(2,1)S(1)}, bf16[2,16,1,16,512]{4,3,1,0,2:T(8,128)(2,1)S(1)}, u32[]{:S(2)}, u32[]{:S(2)}) collective-permute-start(bf16[2,16,1,16,512]{4,3,1,0,2:T(8,128)(2,1)S(1)} %fusion.37), channel_id=1, source_target_pairs={{0,1},{1,0},{2,3},{3,2},{4,5},{5,4},{6,7},{7,6},{8,9},{9,8},{10,11... | collective-permute-start | bytes 1572872 | tf_op jit(solution)/shard_map/ppermute | solution.py:686
  330.0 4.4 %collective-permute-start.4 = (bf16[512,512]{1,0:T(8,128)(2,1)S(1)}, bf16[512,512]{1,0:T(8,128)(2,1)S(1)}, u32[]{:S(2)}, u32[]{:S(2)}) collective-permute-start(bf16[512,512]{1,0:T(8,128)(2,1)S(1)} %copy-done.37), channel_id=1, source_target_pairs={{0,1},{1,0},{2,3},{3,2},{4,5},{5,4},{6,7},{7,6},{8,9},{9,8},{10,11... | collective-permute-start | bytes 1572872 | tf_op jit(solution)/shard_map/ppermute | solution.py:686
  331.8 59.6 %collective-permute-start.52 = (bf16[1,4,2,64,512]{4,3,2,1,0:T(8,128)(2,1)S(1)}, bf16[1,4,2,64,512]{4,3,2,1,0:T(8,128)(2,1)S(1)}, u32[]{:S(2)}, u32[]{:S(2)}) collective-permute-start(bf16[1,4,2,64,512]{4,3,2,1,0:T(8,128)(2,1)S(1)} %dynamic-slice_bitcast_fusion.4), channel_id=1, source_target_pairs={{0,4},{1,5},{2,6},{3,7},{4,0},{5,1},{6,2},{7,3},{8,12},{9,13},{10,... | collective-permute-start | bytes 1572872 | tf_op jit(solution)/shard_map/ppermute | solution.py:686
  333.0 60.0 %collective-permute-start.42 = (bf16[1,8,1,16,2048]{4,3,1,2,0:T(8,128)(2,1)S(1)}, bf16[1,8,1,16,2048]{4,3,1,2,0:T(8,128)(2,1)S(1)}, u32[]{:S(2)}, u32[]{:S(2)}) collective-permute-start(bf16[1,8,1,16,2048]{4,3,1,2,0:T(8,128)(2,1)S(1)} %dynamic-slice_bitcast_fusion.6), channel_id=1, source_target_pairs={{0,2},{1,3},{2,0},{3,1},{4,6},{5,7},{6,4},{7,5},{8,10},{9,11},{10,... | collective-permute-start | bytes 1572872 | tf_op jit(solution)/shard_map/ppermute | solution.py:686
  334.4 18.2 %collective-permute-start.7 = (bf16[2,8,1,16,512]{4,3,1,0,2:T(8,128)(2,1)S(1)}, bf16[2,8,1,16,512]{4,3,1,0,2:T(8,128)(2,1)S(1)}, u32[]{:S(2)}, u32[]{:S(2)}) collective-permute-start(bf16[2,8,1,16,512]{4,3,1,0,2:T(8,128)(2,1)S(1)} %dynamic-slice_bitcast_fusion.15), channel_id=1, source_target_pairs={{0,2},{1,3},{2,0},{3,1},{4,6},{5,7},{6,4},{7,5},{8,10},{9,11},{10,... | collective-permute-start | bytes 786440 | tf_op jit(solution)/shard_map/ppermute | solution.py:686
  335.7 52.5 %copy-start.29 = (f32[2,512,512]{2,1,0:T(8,128)}, f32[2,512,512]{2,1,0:T(8,128)S(1)}, u32[]{:S(2)}) copy-start(f32[2,512,512]{2,1,0:T(8,128)S(1)} %fusion.15) | copy-start | bytes 6291460
  352.6 7.5 %collective-permute-start.12 = (bf16[2,4,2,16,512]{4,3,2,1,0:T(8,128)(2,1)S(1)}, bf16[2,4,2,16,512]{4,3,2,1,0:T(8,128)(2,1)S(1)}, u32[]{:S(2)}, u32[]{:S(2)}) collective-permute-start(bf16[2,4,2,16,512]{4,3,2,1,0:T(8,128)(2,1)S(1)} %dynamic-slice_bitcast_fusion.14), channel_id=1, source_target_pairs={{0,4},{1,5},{2,6},{3,7},{4,0},{5,1},{6,2},{7,3},{8,12},{9,13},{10,... | collective-permute-start | bytes 786440 | tf_op jit(solution)/shard_map/ppermute | solution.py:686
  353.9 34.4 %copy-start.23 = (bf16[2048,512]{1,0:T(8,128)(2,1)S(1)}, bf16[2048,512]{1,0:T(8,128)(2,1)}, u32[]{:S(2)}) copy-start(bf16[2048,512]{1,0:T(8,128)(2,1)} %get-tuple-element.159) | copy-start | bytes 6291460
  360.0 5.0 %collective-permute-start.8 = (bf16[2,4,1,16,512]{4,3,1,0,2:T(8,128)(2,1)S(1)}, bf16[2,4,1,16,512]{4,3,1,0,2:T(8,128)(2,1)S(1)}, u32[]{:S(2)}, u32[]{:S(2)}) collective-permute-start(bf16[2,4,1,16,512]{4,3,1,0,2:T(8,128)(2,1)S(1)} %dynamic-slice_bitcast_fusion.22), channel_id=1, source_target_pairs={{0,4},{1,5},{2,6},{3,7},{4,0},{5,1},{6,2},{7,3},{8,12},{9,13},{10,... | collective-permute-start | bytes 393224 | tf_op jit(solution)/shard_map/ppermute | solution.py:686
  365.0 5.0 %collective-permute-start.13 = (bf16[2,4,1,16,512]{4,3,2,1,0:T(8,128)(2,1)S(1)}, bf16[2,4,1,16,512]{4,3,2,1,0:T(8,128)(2,1)S(1)}, u32[]{:S(2)}, u32[]{:S(2)}) collective-permute-start(bf16[2,4,1,16,512]{4,3,2,1,0:T(8,128)(2,1)S(1)} %constant_dynamic-slice_fusion.15), channel_id=1, source_target_pairs={{0,2},{1,3},{2,0},{3,1},{4,6},{5,7},{6,4},{7,5},{8,10},{9,11},{10,... | collective-permute-start | bytes 393224 | tf_op jit(solution)/shard_map/ppermute | solution.py:686
  370.0 4.3 collective-permute-start.9
  374.2 4.3 collective-permute-start.14
  378.5 4.8 %collective-permute-start.10 = (bf16[2,1,1,16,512]{4,3,1,0,2:T(8,128)(2,1)S(1)}, bf16[2,1,1,16,512]{4,3,1,0,2:T(8,128)(2,1)S(1)}, u32[]{:S(2)}, u32[]{:S(2)}) collective-permute-start(bf16[2,1,1,16,512]{4,3,1,0,2:T(8,128)(2,1)S(1)} %constant_dynamic-slice_fusion.16), channel_id=1, source_target_pairs={{0,16},{1,17},{2,18},{3,19},{4,20},{5,21},{6,22},{7,23},{8,24},{9,... | collective-permute-start | bytes 98312 | tf_op jit(solution)/shard_map/ppermute | solution.py:686
  383.3 4.8 %collective-permute-start.15 = (bf16[2,1,1,16,512]{4,3,2,1,0:T(8,128)(2,1)S(1)}, bf16[2,1,1,16,512]{4,3,2,1,0:T(8,128)(2,1)S(1)}, u32[]{:S(2)}, u32[]{:S(2)}) collective-permute-start(bf16[2,1,1,16,512]{4,3,2,1,0:T(8,128)(2,1)S(1)} %constant_dynamic-slice_fusion.14), channel_id=1, source_target_pairs={{0,16},{1,17},{2,18},{3,19},{4,20},{5,21},{6,22},{7,23},{8,24},{9,... | collective-permute-start | bytes 98312 | tf_op jit(solution)/shard_map/ppermute | solution.py:686
  390.1 24.7 %collective-permute-start.47 = (bf16[1,4,2,64,512]{4,3,2,1,0:T(8,128)(2,1)S(1)}, bf16[1,4,2,64,512]{4,3,2,1,0:T(8,128)(2,1)S(1)}, u32[]{:S(2)}, u32[]{:S(2)}) collective-permute-start(bf16[1,4,2,64,512]{4,3,2,1,0:T(8,128)(2,1)S(1)} %dynamic-slice_bitcast_fusion.5), channel_id=1, source_target_pairs={{0,4},{1,5},{2,6},{3,7},{4,0},{5,1},{6,2},{7,3},{8,12},{9,13},{10,... | collective-permute-start | bytes 1572872 | tf_op jit(solution)/shard_map/ppermute | solution.py:686
  391.6 11.9 %collective-permute-start.53 = (bf16[1,4,1,64,512]{4,3,2,1,0:T(8,128)(2,1)S(1)}, bf16[1,4,1,64,512]{4,3,2,1,0:T(8,128)(2,1)S(1)}, u32[]{:S(2)}, u32[]{:S(2)}) collective-permute-start(bf16[1,4,1,64,512]{4,3,2,1,0:T(8,128)(2,1)S(1)} %constant_dynamic-slice_fusion.2), channel_id=1, source_target_pairs={{0,2},{1,3},{2,0},{3,1},{4,6},{5,7},{6,4},{7,5},{8,10},{9,11},{10,... | collective-permute-start | bytes 786440 | tf_op jit(solution)/shard_map/ppermute | solution.py:686
  393.2 9.0 %collective-permute-start.43 = (bf16[1,4,1,16,2048]{4,3,1,2,0:T(8,128)(2,1)S(1)}, bf16[1,4,1,16,2048]{4,3,1,2,0:T(8,128)(2,1)S(1)}, u32[]{:S(2)}, u32[]{:S(2)}) collective-permute-start(bf16[1,4,1,16,2048]{4,3,1,2,0:T(8,128)(2,1)S(1)} %dynamic-slice_bitcast_fusion.8), channel_id=1, source_target_pairs={{0,4},{1,5},{2,6},{3,7},{4,0},{5,1},{6,2},{7,3},{8,12},{9,13},{10,... | collective-permute-start | bytes 786440 | tf_op jit(solution)/shard_map/ppermute | solution.py:686
  394.3 22.4 %collective-permute-start.37 = (bf16[1,8,1,16,2048]{4,3,1,2,0:T(8,128)(2,1)S(1)}, bf16[1,8,1,16,2048]{4,3,1,2,0:T(8,128)(2,1)S(1)}, u32[]{:S(2)}, u32[]{:S(2)}) collective-permute-start(bf16[1,8,1,16,2048]{4,3,1,2,0:T(8,128)(2,1)S(1)} %dynamic-slice_bitcast_fusion.7), channel_id=1, source_target_pairs={{0,2},{1,3},{2,0},{3,1},{4,6},{5,7},{6,4},{7,5},{8,10},{9,11},{10,... | collective-permute-start | bytes 1572872 | tf_op jit(solution)/shard_map/ppermute | solution.py:686
  402.2 5.0 %collective-permute-start.44 = (bf16[1,2,1,16,2048]{4,3,2,1,0:T(8,128)(2,1)S(1)}, bf16[1,2,1,16,2048]{4,3,2,1,0:T(8,128)(2,1)S(1)}, u32[]{:S(2)}, u32[]{:S(2)}) collective-permute-start(bf16[1,2,1,16,2048]{4,3,2,1,0:T(8,128)(2,1)S(1)} %dynamic-slice_bitcast_fusion.18), channel_id=1, source_target_pairs={{0,8},{1,9},{2,10},{3,11},{4,12},{5,13},{6,14},{7,15},{8,0},{9,1},... | collective-permute-start | bytes 393224 | tf_op jit(solution)/shard_map/ppermute | solution.py:686
  403.6 5.8 %collective-permute-start.54 = (bf16[1,2,1,64,512]{4,3,2,1,0:T(8,128)(2,1)S(1)}, bf16[1,2,1,64,512]{4,3,2,1,0:T(8,128)(2,1)S(1)}, u32[]{:S(2)}, u32[]{:S(2)}) collective-permute-start(bf16[1,2,1,64,512]{4,3,2,1,0:T(8,128)(2,1)S(1)} %dynamic-slice_bitcast_fusion.16), channel_id=1, source_target_pairs={{0,8},{1,9},{2,10},{3,11},{4,12},{5,13},{6,14},{7,15},{8,0},{9,1},... | collective-permute-start | bytes 393224 | tf_op jit(solution)/shard_map/ppermute | solution.py:686
  407.3 5.9 %collective-permute-start.45 = (bf16[1,1,1,16,2048]{4,3,2,1,0:T(8,128)(2,1)S(1)}, bf16[1,1,1,16,2048]{4,3,2,1,0:T(8,128)(2,1)S(1)}, u32[]{:S(2)}, u32[]{:S(2)}) collective-permute-start(bf16[1,1,1,16,2048]{4,3,2,1,0:T(8,128)(2,1)S(1)} %constant_dynamic-slice_fusion.5), channel_id=1, source_target_pairs={{0,16},{1,17},{2,18},{3,19},{4,20},{5,21},{6,22},{7,23},{8,24},{9,... | collective-permute-start | bytes 196616 | tf_op jit(solution)/shard_map/ppermute | solution.py:686
  409.5 5.3 %collective-permute-start.55 = (bf16[1,1,1,64,512]{4,3,2,1,0:T(8,128)(2,1)S(1)}, bf16[1,1,1,64,512]{4,3,2,1,0:T(8,128)(2,1)S(1)}, u32[]{:S(2)}, u32[]{:S(2)}) collective-permute-start(bf16[1,1,1,64,512]{4,3,2,1,0:T(8,128)(2,1)S(1)} %constant_dynamic-slice_fusion.1), channel_id=1, source_target_pairs={{0,16},{1,17},{2,18},{3,19},{4,20},{5,21},{6,22},{7,23},{8,24},{9,... | collective-permute-start | bytes 196616 | tf_op jit(solution)/shard_map/ppermute | solution.py:686
  415.0 6.4 %collective-permute-start.48 = (bf16[1,4,1,64,512]{4,3,2,1,0:T(8,128)(2,1)S(1)}, bf16[1,4,1,64,512]{4,3,2,1,0:T(8,128)(2,1)S(1)}, u32[]{:S(2)}, u32[]{:S(2)}) collective-permute-start(bf16[1,4,1,64,512]{4,3,2,1,0:T(8,128)(2,1)S(1)} %constant_dynamic-slice_fusion.4), channel_id=1, source_target_pairs={{0,2},{1,3},{2,0},{3,1},{4,6},{5,7},{6,4},{7,5},{8,10},{9,11},{10,... | collective-permute-start | bytes 786440 | tf_op jit(solution)/shard_map/ppermute | solution.py:686
  416.9 7.3 %collective-permute-start.38 = (bf16[1,4,1,16,2048]{4,3,1,2,0:T(8,128)(2,1)S(1)}, bf16[1,4,1,16,2048]{4,3,1,2,0:T(8,128)(2,1)S(1)}, u32[]{:S(2)}, u32[]{:S(2)}) collective-permute-start(bf16[1,4,1,16,2048]{4,3,1,2,0:T(8,128)(2,1)S(1)} %dynamic-slice_bitcast_fusion.9), channel_id=1, source_target_pairs={{0,4},{1,5},{2,6},{3,7},{4,0},{5,1},{6,2},{7,3},{8,12},{9,13},{10,... | collective-permute-start | bytes 786440 | tf_op jit(solution)/shard_map/ppermute | solution.py:686
  421.6 5.6 %collective-permute-start.49 = (bf16[1,2,1,64,512]{4,3,1,2,0:T(8,128)(2,1)S(1)}, bf16[1,2,1,64,512]{4,3,1,2,0:T(8,128)(2,1)S(1)}, u32[]{:S(2)}, u32[]{:S(2)}) collective-permute-start(bf16[1,2,1,64,512]{4,3,1,2,0:T(8,128)(2,1)S(1)} %dynamic-slice_bitcast_fusion.17), channel_id=1, source_target_pairs={{0,8},{1,9},{2,10},{3,11},{4,12},{5,13},{6,14},{7,15},{8,0},{9,1},... | collective-permute-start | bytes 393224 | tf_op jit(solution)/shard_map/ppermute | solution.py:686
  424.3 5.2 %collective-permute-start.39 = (bf16[1,2,1,16,2048]{4,3,1,2,0:T(8,128)(2,1)S(1)}, bf16[1,2,1,16,2048]{4,3,1,2,0:T(8,128)(2,1)S(1)}, u32[]{:S(2)}, u32[]{:S(2)}) collective-permute-start(bf16[1,2,1,16,2048]{4,3,1,2,0:T(8,128)(2,1)S(1)} %dynamic-slice_bitcast_fusion.19), channel_id=1, source_target_pairs={{0,8},{1,9},{2,10},{3,11},{4,12},{5,13},{6,14},{7,15},{8,0},{9,1},... | collective-permute-start | bytes 393224 | tf_op jit(solution)/shard_map/ppermute | solution.py:686
  427.2 5.2 %collective-permute-start.50 = (bf16[1,1,1,64,512]{4,3,1,2,0:T(8,128)(2,1)S(1)}, bf16[1,1,1,64,512]{4,3,1,2,0:T(8,128)(2,1)S(1)}, u32[]{:S(2)}, u32[]{:S(2)}) collective-permute-start(bf16[1,1,1,64,512]{4,3,1,2,0:T(8,128)(2,1)S(1)} %constant_dynamic-slice_fusion.3), channel_id=1, source_target_pairs={{0,16},{1,17},{2,18},{3,19},{4,20},{5,21},{6,22},{7,23},{8,24},{9,... | collective-permute-start | bytes 196616 | tf_op jit(solution)/shard_map/ppermute | solution.py:686
  429.5 5.2 %collective-permute-start.40 = (bf16[1,1,1,16,2048]{4,3,1,2,0:T(8,128)(2,1)S(1)}, bf16[1,1,1,16,2048]{4,3,1,2,0:T(8,128)(2,1)S(1)}, u32[]{:S(2)}, u32[]{:S(2)}) collective-permute-start(bf16[1,1,1,16,2048]{4,3,1,2,0:T(8,128)(2,1)S(1)} %constant_dynamic-slice_fusion.6), channel_id=1, source_target_pairs={{0,16},{1,17},{2,18},{3,19},{4,20},{5,21},{6,22},{7,23},{8,24},{9,... | collective-permute-start | bytes 196616 | tf_op jit(solution)/shard_map/ppermute | solution.py:686
  (35 other events, 227.8 us)
